TPU v7x, 32 devices: a whole 2x2x4 slice. The times are simulated.
32 devices in a mesh: groups: 2 (over x), seq: 16 (over z, y, core).
Axes of the slice: x: 2, y: 2, z: 4, core: 2. Of those that a mesh axis runs over, the one named last changes fastest.
Arguments:
- activations: bfloat16 [512, 14336], P(('groups', 'seq')), parts along dimension 0, may hold values from -6 to 6
- out_grads: bfloat16 [512, 2048], P(('groups', 'seq')), parts along dimension 0, may hold values from -6 to 6
- query_ids: int32 [512], P(('groups', 'seq')), parts along dimension 0, may hold values from 0 to 2, never falling along the last dimension, each value on 1 to 128 neighbouring positions
- act_basis: bfloat16 [64, 224, 224], P('seq'), may hold values from -0.375 to 0.375
- grad_basis: bfloat16 [2048, 2048], P(None, 'seq'), may hold values from -0.125 to 0.125
- eigenvalues: float32 [2048, 14336], P(None, 'seq'), may hold values from 8 to 80
Outputs:
- precond: bfloat16 [6, 2048, 14336], P('groups', None, 'seq'), parts along dimension 0
There are 2 independent parts, one for each index of `groups`. A program takes and returns all parts, laid end to end along the dimension named above; an argument that names none is the same for every part. Nothing has to cross between parts.
Inputs may be any that keep to these rules, and one draw needn't show every extreme that they name: `query_ids`: query ids never fall along the tokens; each of the 3 queries has at least one and at most 128 tokens.
All inputs are finite; a program needn't handle non-finite values.
Results may differ from a plain program's by a relative error of at most 0.006.
Values may be sent and summed in bfloat16 or wider, within the bound.
No kernel may reach another device: no remote copies, remote signals or barrier semaphores. Data moves between devices by JAX's collectives and lax.ppermute only.
A program may use at most 128 MiB of HBM per device.

v0:
```python
import jax
import jax.numpy as jnp
from jax import lax
from jax.sharding import PartitionSpec as P

QUERIES = 3


def shards(activations, out_grads, query_ids, act_basis, grad_basis, eigenvalues):
    local_blocks = act_basis.shape[0]
    block_order = act_basis.shape[1]
    out_units = grad_basis.shape[0]
    columns = lax.all_to_all(activations, "seq", split_axis=1, concat_axis=0, tiled=True)
    all_tokens = columns.shape[0]
    local_width = local_blocks * block_order
    rotated_act = jnp.einsum(
        "tbi,bik->tbk",
        columns.reshape(all_tokens, local_blocks, block_order),
        act_basis,
        preferred_element_type=jnp.float32,
    )
    rotated_act = rotated_act.astype(jnp.bfloat16).reshape(all_tokens, local_width)
    full_basis = lax.all_gather(grad_basis, "seq", axis=1, tiled=True)
    own_rotated = jnp.dot(out_grads, full_basis, preferred_element_type=jnp.float32).astype(
        jnp.bfloat16
    )
    rotated_grad, token_query = (
        lax.all_gather(own_rotated, "seq", axis=0, tiled=True),
        lax.all_gather(query_ids, "seq", axis=0, tiled=True),
    )
    selector = (token_query[:, None] == jnp.arange(QUERIES, dtype=jnp.int32)[None, :]).astype(
        jnp.bfloat16
    )
    selected = (rotated_act[:, None, :] * selector[:, :, None]).reshape(
        all_tokens, QUERIES * local_width
    )
    moments = lax.dot_general(
        rotated_grad, selected, (((0,), (0,)), ((), ())), preferred_element_type=jnp.float32
    )
    scaled = (moments.reshape(out_units, QUERIES, local_width) / eigenvalues[:, None, :]).astype(
        jnp.bfloat16
    )
    rotated_back = jnp.einsum(
        "dqbk,bik->dqbi",
        scaled.reshape(out_units, QUERIES, local_blocks, block_order),
        act_basis,
        preferred_element_type=jnp.float32,
    )
    rotated_back = rotated_back.astype(jnp.bfloat16).reshape(out_units, QUERIES * local_width)
    result = jnp.dot(full_basis, rotated_back, preferred_element_type=jnp.float32)
    result = result.reshape(out_units, QUERIES, local_width)
    return jnp.transpose(result, (1, 0, 2)).astype(jnp.bfloat16)


def solution(mesh):
    return jax.shard_map(
        shards,
        mesh=mesh,
        in_specs=(
            P(("groups", "seq"), None),
            P(("groups", "seq"), None),
            P(("groups", "seq")),
            P("seq", None, None),
            P(None, "seq"),
            P(None, "seq"),
        ),
        out_specs=P("groups", None, "seq"),
        check_vma=False,
    )
```

profile of v0, /device:TPU:0, one launch (start us, length us, event | category | flops | bytes accessed | tf_op | source)
XLA Modules:
  0.0 207.3 jit_solution(7658103903438815733)
XLA Ops:
  6.5 0.0 copy-start
  6.5 0.0 all-gather.3.cloned.1.call-start
  6.5 0.7 all-gather.3.cloned.1.call-update
  7.3 0.0 all-gather.5.cloned.1.call-start
  7.3 82.6 %all-gather.3.cloned.1.call-done = bf16[2048,2048]{1,0:T(8,128)(2,1)} async-done(((bf16[2048,128]{1,0:T(8,128)(2,1)}), bf16[2048,2048]{1,0:T(8,128)(2,1)}) %all-gather.3.cloned.1.call-update) | async-done | bytes 8388624 | tf_op jit(solution)/shard_map/all_gather | solution.py:23
  90.0 5.2 %convolution_convert_fusion.1 = bf16[16,2048]{1,0:T(8,128)(2,1)} fusion(bf16[16,2048]{1,0:T(8,128)(2,1)} %param.7, bf16[2048,2048]{1,0:T(8,128)(2,1)} %all-gather.3.cloned.1.call-done), kind=kOutput, calls=%fused_computation.5 | convolution fusion | flops 134250496 | bytes 8519680 | tf_op jit(solution)/shard_map/dot_general | solution.py:24
  95.2 0.0 all-gather.5.cloned.1.call-update
  95.2 0.8 copy.29
  96.0 3.6 %all-to-all-start = ((bf16[16,16,896]{2,0,1:T(8,128)(2,1)}), bf16[16,16,896]{2,0,1:T(8,128)(2,1)S(1)}, u32[]{:S(2)}, u32[]{:S(2)}) async-start(bf16[16,16,896]{2,0,1:T(8,128)(2,1)} %bitcast.36), calls=%async_computation | async-start | bytes 917504 | tf_op jit(solution)/shard_map/all_to_all | solution.py:13
  99.6 8.6 %copy.15 = f32[2048,896]{0,1:T(8,128)} copy(f32[2048,896]{1,0:T(8,128)} %param.11) | data formatting | bytes 14680064 | tf_op args[5]
  108.2 0.0 copy-done.4
  108.2 0.6 dynamic-slice
  109.4 0.0 copy-done.3
  109.4 0.2 dynamic-update-slice
  109.6 12.4 %all-reduce = s32[256]{0:T(256)S(1)} all-reduce(s32[256]{0:T(256)S(1)} %dynamic-update-slice), channel_id=1, replica_groups=mesh['groups'=2,'seq'=16] {'seq'}, use_global_device_ids=true, to_apply=%add | all-reduce | flops 256 | bytes 2048
  122.1 0.0 all-to-all-done
  122.1 0.5 reshape.45
  122.6 0.3 convolution_convert_fusion.2
  122.9 10.5 %all-gather.5.cloned.1.call-done = bf16[256,2048]{1,0:T(8,128)(2,1)} async-done(((bf16[16,2048]{1,0:T(8,128)(2,1)}), bf16[256,2048]{1,0:T(8,128)(2,1)}) %all-gather.5.cloned.1.call-update) | async-done | bytes 1048592 | tf_op jit(solution)/shard_map/all_gather | solution.py:28
  133.5 8.2 %divide_convert_fusion = bf16[2048,3,896]{0,2,1:T(8,128)(2,1)} fusion(f32[2048,896]{0,1:T(8,128)} %copy.15, bf16[256,2048]{1,0:T(8,128)(2,1)} %all-gather.5.cloned.1.call-done, bf16[256,3]{0,1:T(4,128)(2,1)S(1)} %fusion.11, bf16[256,896]{0,1:T(8,128)(2,1)S(1)} %bitcast.42), kind=kOutput, calls=%fused_computation | convolution fusion | flops 2832334848 | bytes 19858944 | tf_op jit(solution)/shard_map/dot_general | solution.py:37
  141.6 11.3 %convert_bitcast_fusion = bf16[2048,3,4,224]{0,3,1,2:T(8,128)(2,1)} fusion(bf16[2048,3,4,224]{0,3,2,1:T(8,128)(2,1)} %bitcast.37, bf16[4,224,224]{2,1,0:T(8,128)(2,1)S(1)} %copy-done), kind=kOutput, calls=%fused_computation.4 | convolution fusion | flops 2471755776 | bytes 22421504 | tf_op jit(solution)/shard_map/dqbk,bik->dqbi/dot_general | solution.py:43
  153.0 5.8 %copy.17 = bf16[2048,3,4,224]{0,3,2,1:T(8,128)(2,1)S(1)} copy(bf16[2048,3,4,224]{0,3,1,2:T(8,128)(2,1)} %convert_bitcast_fusion) | data formatting | bytes 22020096 | tf_op jit(solution)/shard_map/convert_element_type | solution.py:49
  158.8 27.0 %convolution_convert_fusion = bf16[2688,2048]{1,0:T(8,128)(2,1)} fusion(bf16[2048,2688]{0,1:T(8,128)(2,1)S(1)} %bitcast.38, bf16[2048,2048]{1,0:T(8,128)(2,1)} %all-gather.3.cloned.1.call-done), kind=kOutput, calls=%fused_computation.1 | convolution fusion | flops 22554083328 | bytes 30408704 | tf_op jit(solution)/shard_map/dot_general | solution.py:50
  185.8 14.7 %copy.18 = bf16[2048,3,896]{2,0,1:T(8,128)(2,1)} copy(bf16[2048,3,896]{0,2,1:T(8,128)(2,1)} %bitcast.39) | data formatting | bytes 22020096 | tf_op jit(solution)/shard_map/convert_element_type | solution.py:52
  (9 shorter events, 0.0 us)
Async XLA Ops:
  6.5 116.0 %copy-start = (bf16[4,224,224]{2,1,0:T(8,128)(2,1)S(1)}, bf16[4,224,224]{2,1,0:T(8,128)(2,1)}, u32[]{:S(2)}) copy-start(bf16[4,224,224]{2,1,0:T(8,128)(2,1)} %param.9) | copy-start | bytes 1204228
  6.5 88.7 %copy-start.2 = (bf16[16,14336]{1,0:T(8,128)(2,1)S(1)}, bf16[16,14336]{1,0:T(8,128)(2,1)}, u32[]{:S(2)}) copy-start(bf16[16,14336]{1,0:T(8,128)(2,1)} %param.6) | copy-start | bytes 1376260
  6.5 83.4 %all-gather.3.cloned.1.call-start = ((), (), s32[]{:S(2)}) async-start(), calls=%async_computation.1 | async-start | bytes 8912896 | tf_op jit(solution)/shard_map/all_gather | solution.py:23
  7.3 126.2 %all-gather.5.cloned.1.call-start = ((), (), s32[]{:S(2)}) async-start(), calls=%async_computation.2 | async-start | bytes 1114112 | tf_op jit(solution)/shard_map/all_gather | solution.py:28
  95.2 13.0 %copy-start.4 = (u32[32]{0:T(128)S(1)}, u32[32]{0:T(128)}, u32[]{:S(2)}) copy-start(u32[32]{0:T(128)} %constant.6) | copy-start | bytes 388
  95.2 14.2 %copy-start.3 = (s32[16]{0:T(128)S(1)}, s32[16]{0:T(128)}, u32[]{:S(2)}) copy-start(s32[16]{0:T(128)} %param.8) | copy-start | bytes 196
  96.0 26.0 %all-to-all-start = ((bf16[16,16,896]{2,0,1:T(8,128)(2,1)}), bf16[16,16,896]{2,0,1:T(8,128)(2,1)S(1)}, u32[]{:S(2)}, u32[]{:S(2)}) async-start(bf16[16,16,896]{2,0,1:T(8,128)(2,1)} %bitcast.36), calls=%async_computation | async-start | bytes 917504 | tf_op jit(solution)/shard_map/all_to_all | solution.py:13
  185.8 14.7 %copy-start.1 = (bf16[4,224,224]{2,1,0:T(8,128)(2,1)S(1)}, bf16[4,224,224]{2,1,0:T(8,128)(2,1)}, u32[]{:S(2)}) copy-start(bf16[4,224,224]{2,1,0:T(8,128)(2,1)} %param.9) | copy-start | bytes 1204228
Sparse Core Ops, SparseCore 0:
  9.5 80.4 all-gather.2
  95.3 38.0 all-gather.4
where the time goes:
time: 208 us; the launch traced here: 207 us
  waiting for transfers between devices  93.9 us (45%)
  matrix products  52.1 us (25%)
  local copies, waits for them, and re-layouts  31.2 us (15%)
  between operations  14 us (7%)
  blocking collectives  12.4 us (6%)
  starting transfers between devices  3.6 us (2%)
    all_gather x1, waiting for transfers between devices, shards(): full_basis = lax.all_gather(grad_basis, 'seq', axis=1, tiled=True)  82.6 us
    dot_general x1, matrix products, shards(): jnp.dot(full_basis, rotated_back, preferred_element_type=jnp.float32)  27 us
    convert_element_type x1, local copies, waits for them, and re-layouts, shards(): return jnp.transpose(result, (1, 0, 2)).astype(jnp.bfloat16)  14.7 us
    unnamed x1, blocking collectives  12.4 us
    dot_general x1, matrix products, shards(): jnp.einsum('dqbk,bik->dqbi', scaled.reshape(out_units, QUERIES, local_blo...  11.3 us
    all_gather x1, waiting for transfers between devices, shards(): lax.all_gather(own_rotated, 'seq', axis=0, tiled=True)  10.5 us
    unnamed x14, local copies, waits for them, and re-layouts  9.46 us
    dot_general x1, matrix products, shards(): lax.dot_general(rotated_grad, selected, (((0,), (0,)), ((), ())), preferr...  8.18 us
  transfers between devices with their start and end apart: 3, of which 2 were waited for; matrix products, arithmetic and copies ran while one was open for 5% of the time, Pallas kernels for 0%

commit v1 on v0

v1 whole, which is shorter than its diff:
```python
import functools

import jax
import jax.numpy as jnp
from jax import lax
from jax.experimental import pallas as pl
from jax.experimental.pallas import tpu as pltpu
from jax.sharding import Mesh
from jax.sharding import PartitionSpec as P

QUERIES = 3
LANES = 128
AXES = ("g", "z", "y", "c")


def windows(width, order):
    out = []
    for n0 in range(0, width, 2 * LANES):
        n1 = min(n0 + 2 * LANES, width)
        k0 = (n0 // order) * order // LANES * LANES
        k1 = min(width, -(-((n1 - 1) // order + 1) * order // LANES) * LANES)
        out.append((n0, n1, k0, k1))
    return out


def level_kernel(order, first, *refs):
    ids_ref = refs[0]
    og_ref, sel_ref, wt_ref = refs[1:4]
    basis_refs = refs[4:8]
    eig_refs = refs[8:12]
    if first:
        acc_ref = None
        out_ref, rb_ref = refs[12:]
    else:
        acc_ref, out_ref, rb_ref = refs[12:]
    del ids_ref
    step = pl.program_id(0)
    rows = out_ref.shape[1]
    width = out_ref.shape[2]
    shard = basis_refs[0].shape[1]

    @pl.when(step == 0)
    def _():
        for pair in range(2):
            basis = jnp.concatenate([r[...] for r in basis_refs[2 * pair : 2 * pair + 2]], axis=1)
            rg = jnp.dot(og_ref[...], basis, preferred_element_type=jnp.float32)
            rgt = rg.astype(jnp.bfloat16).T
            inv = 1.0 / jnp.concatenate([r[...] for r in eig_refs[2 * pair : 2 * pair + 2]], axis=0)
            for q in range(QUERIES):
                m = jnp.dot(rgt, sel_ref[q], preferred_element_type=jnp.float32)
                s = (m * inv).astype(jnp.bfloat16)
                for n0, n1, k0, k1 in windows(width, order):
                    back = jnp.dot(
                        s[:, k0:k1], wt_ref[k0:k1, n0:n1], preferred_element_type=jnp.float32
                    )
                    rb_ref[q, 2 * pair * shard : 2 * (pair + 1) * shard, n0:n1] = back.astype(
                        jnp.bfloat16
                    )

    at = pl.ds(pl.multiple_of(step * rows, rows), rows)
    lhs = jnp.concatenate([r[at, :] for r in basis_refs], axis=1)
    for q in range(QUERIES):
        part = jnp.dot(lhs, rb_ref[q], preferred_element_type=jnp.float32)
        if not first:
            part = part + acc_ref[q].astype(jnp.float32)
        out_ref[q] = part.astype(jnp.bfloat16)


def level(order, shard_ids, og, sel, wt, bases, eig, acc):
    units = og.shape[1]
    width = sel.shape[2]
    shard = bases[0].shape[1]
    rows = 2 * LANES
    first = acc is None
    const2 = lambda i, s: (0, 0)
    one = pl.Buffered(1)
    in_specs = [
        pl.BlockSpec(og.shape, const2, pipeline_mode=one),
        pl.BlockSpec(sel.shape, lambda i, s: (0, 0, 0), pipeline_mode=one),
        pl.BlockSpec(wt.shape, const2, pipeline_mode=one),
    ]
    in_specs += [pl.BlockSpec(bases[0].shape, const2, pipeline_mode=one)] * 4
    for j in range(4):
        in_specs.append(
            pl.BlockSpec((shard, width), lambda i, s, j=j: (s[j], 0), pipeline_mode=one)
        )
    out_block = pl.BlockSpec((QUERIES, rows, width), lambda i, s: (0, i, 0))
    args = [og, sel, wt, *bases, eig, eig, eig, eig]
    if not first:
        in_specs.append(out_block)
        args.append(acc)
    flops = 2 * QUERIES * width * 4 * shard * units
    return pl.pallas_call(
        functools.partial(level_kernel, order, first),
        out_shape=jax.ShapeDtypeStruct((QUERIES, units, width), jnp.bfloat16),
        grid_spec=pltpu.PrefetchScalarGridSpec(
            num_scalar_prefetch=1,
            grid=(units // rows,),
            in_specs=in_specs,
            out_specs=out_block,
            scratch_shapes=[pltpu.VMEM((QUERIES, 4 * shard, width), jnp.bfloat16)],
        ),
        input_output_aliases={} if first else {len(args): 0},
        compiler_params=pltpu.CompilerParams(
            dimension_semantics=("arbitrary",), vmem_limit_bytes=36 << 20
        ),
        cost_estimate=pl.CostEstimate(
            flops=flops, bytes_accessed=2 * QUERIES * units * width * 2, transcendentals=0
        ),
        name="level_first" if first else "level_next",
    )(shard_ids, *args)


def block_diagonal(blocks):
    count, order, _ = blocks.shape
    rows = [
        jnp.pad(blocks[b], ((0, 0), (b * order, (count - 1 - b) * order))) for b in range(count)
    ]
    return jnp.concatenate(rows, axis=0)


def ring_of(nz):
    return [0] + list(range(1, nz, 2)) + [z for z in range(nz - 1, 0, -1) if z % 2 == 0]


def streamed(shape, activations, out_grads, query_ids, act_basis, grad_basis, eigenvalues):
    ng, nz, ny, nc = shape
    count, order, _ = act_basis.shape
    width = count * order
    tokens = activations.shape[0]
    chips = nz * ny
    units = grad_basis.shape[0]

    def enc(g, z, y, c):
        return ((g * nz + z) * ny + y) * nc + c

    every = [
        (g, z, y, c) for g in range(ng) for z in range(nz) for y in range(ny) for c in range(nc)
    ]
    order_z = ring_of(nz)
    follow = {z: order_z[(i + 1) % nz] for i, z in enumerate(order_z)}
    before = {v: k for k, v in follow.items()}
    perm_core = [(enc(g, z, y, c), enc(g, z, y, 1 - c)) for g, z, y, c in every]
    perm_y = [(enc(g, z, y, c), enc(g, z, 1 - y, c)) for g, z, y, c in every]
    perm_z = [(enc(g, z, y, c), enc(g, follow[z], y, c)) for g, z, y, c in every]
    move = lambda v, p: lax.ppermute(v, AXES, p)

    ids = jnp.broadcast_to(query_ids.astype(jnp.bfloat16)[:, None], (tokens, LANES))
    common = jnp.concatenate([out_grads, ids], axis=1)
    parcels = jnp.concatenate(
        [
            activations.reshape(tokens, chips, nc * width).transpose(1, 0, 2),
            jnp.broadcast_to(common[None], (chips,) + common.shape),
        ],
        axis=2,
    )
    got = lax.all_to_all(parcels, ("z", "y"), split_axis=0, concat_axis=0, tiled=True)
    got = got.reshape(chips * tokens, nc * width + units + LANES)
    core = lax.axis_index("c")
    low, high, shared = got[:, :width], got[:, width : 2 * width], got[:, 2 * width :]
    mine = jnp.where(core == 0, low, high)
    other = jnp.where(core == 0, high, low)
    swapped = move(jnp.concatenate([other, shared], axis=1), perm_core)
    columns = jnp.concatenate([mine, swapped[:, :width]], axis=0)
    grads = jnp.concatenate([shared, swapped[:, width:]], axis=0)
    og, token_query = grads[:, :units], grads[:, units]

    levels = []
    own = grad_basis
    for k in range(nz):
        if k:
            own = move(own, perm_z)
        across = move(own, perm_y)
        levels.append((own, across, move(own, perm_core), move(across, perm_core)))

    rotated_act = jnp.dot(
        columns, block_diagonal(act_basis), preferred_element_type=jnp.float32
    ).astype(jnp.bfloat16)
    zero = jnp.zeros((), jnp.bfloat16)
    sel = jnp.stack(
        [
            jnp.where((token_query == jnp.bfloat16(q))[:, None], rotated_act, zero)
            for q in range(QUERIES)
        ]
    )
    wt = block_diagonal(jnp.swapaxes(act_basis, 1, 2))

    z, y, c = lax.axis_index("z"), lax.axis_index("y"), lax.axis_index("c")
    acc = None
    level_z = list(range(nz))
    for k in range(nz):
        zk = jnp.asarray(level_z, jnp.int32)[z]
        shard_ids = jnp.stack(
            [(zk * ny + yy) * nc + cc for cc in (c, 1 - c) for yy in (y, 1 - y)]
        ).astype(jnp.int32)
        acc = level(order, shard_ids, og, sel, wt, levels[k], eigenvalues, acc)
        level_z = [before[v] for v in level_z]
    return acc


def plain(activations, out_grads, query_ids, act_basis, grad_basis, eigenvalues):
    local_blocks, block_order = act_basis.shape[:2]
    out_units = grad_basis.shape[0]
    columns = lax.all_to_all(activations, AXES[1:], split_axis=1, concat_axis=0, tiled=True)
    all_tokens = columns.shape[0]
    local_width = local_blocks * block_order
    rotated_act = jnp.einsum(
        "tbi,bik->tbk",
        columns.reshape(all_tokens, local_blocks, block_order),
        act_basis,
        preferred_element_type=jnp.float32,
    )
    rotated_act = rotated_act.astype(jnp.bfloat16).reshape(all_tokens, local_width)
    full_basis = lax.all_gather(grad_basis, AXES[1:], axis=1, tiled=True)
    own_rotated = jnp.dot(out_grads, full_basis, preferred_element_type=jnp.float32).astype(
        jnp.bfloat16
    )
    rotated_grad = lax.all_gather(own_rotated, AXES[1:], axis=0, tiled=True)
    token_query = lax.all_gather(query_ids, AXES[1:], axis=0, tiled=True)
    selector = (token_query[:, None] == jnp.arange(QUERIES, dtype=jnp.int32)[None, :]).astype(
        jnp.bfloat16
    )
    results = []
    for q in range(QUERIES):
        moments = lax.dot_general(
            rotated_grad,
            rotated_act * selector[:, q : q + 1],
            (((0,), (0,)), ((), ())),
            preferred_element_type=jnp.float32,
        )
        scaled = (moments / eigenvalues).astype(jnp.bfloat16)
        back = jnp.einsum(
            "dbk,bik->dbi",
            scaled.reshape(out_units, local_blocks, block_order),
            act_basis,
            preferred_element_type=jnp.float32,
        )
        back = back.astype(jnp.bfloat16).reshape(out_units, local_width)
        results.append(
            jnp.dot(full_basis, back, preferred_element_type=jnp.float32).astype(jnp.bfloat16)
        )
    return jnp.stack(results, axis=0)


def solution(mesh):
    ng, ns = mesh.shape["groups"], mesh.shape["seq"]
    ny = nc = 2
    nz = ns // (ny * nc)
    shape = (ng, nz, ny, nc)
    fine = Mesh(mesh.devices.reshape(shape), AXES)
    seq = AXES[1:]

    def body(activations, out_grads, query_ids, act_basis, grad_basis, eigenvalues):
        shard = grad_basis.shape[1]
        width = act_basis.shape[0] * act_basis.shape[1]
        if shard % LANES or width % LANES or nz % 2:
            return plain(activations, out_grads, query_ids, act_basis, grad_basis, eigenvalues)
        return streamed(
            shape, activations, out_grads, query_ids, act_basis, grad_basis, eigenvalues
        )

    return jax.shard_map(
        body,
        mesh=fine,
        in_specs=(
            P(AXES, None),
            P(AXES, None),
            P(AXES),
            P(seq, None, None),
            P(None, seq),
            P(None, seq),
        ),
        out_specs=P("g", None, seq),
        check_vma=False,
    )
```

time: 208 us -> 150 us (0.72)
  Pallas kernels: 0 us -> 70 us
  waiting for transfers between devices: 93.9 us -> 41.2 us
  matrix products: 52.1 us -> 0.8 us
  local copies, waits for them, and re-layouts: 31.2 us -> 7.61 us
  starting transfers between devices: 3.6 us -> 16.8 us
  blocking collectives: 12.4 us -> 0 us
  between operations: 14 us -> 2.16 us
  other arithmetic: 0.01 us -> 9.92 us
    all_gather x2 -> x0, waiting for transfers between devices: 93.2 us -> none  [the longest x1 82.6 us: shards(): full_basis = lax.all_gather(grad_basis, 'seq', axis=1, tiled=True)]
    pallas_call x0 -> x4, Pallas kernels: none -> 70 us  [level(): pl.pallas_call(functools.partial(level_kernel, order, first), out_shape=j...]
    dot_general x5 -> x1, matrix products: 52.1 us -> 0.8 us  [streamed(): jnp.dot(columns, block_diagonal(act_basis), preferred_element_type=jnp.fl...]
    ppermute x0 -> x16, waiting for transfers between devices: none -> 26 us  [streamed(): move = lambda v, p: lax.ppermute(v, AXES, p)]
    convert_element_type x2 -> x0, local copies, waits for them, and re-layouts: 20.5 us -> none  [the longest x1 14.7 us: shards(): return jnp.transpose(result, (1, 0, 2)).astype(jnp.bfloat16)]
    all_to_all x1, waiting for transfers between devices: 0.01 us -> 15.2 us  [streamed(): lax.all_to_all(parcels, ('z', 'y'), split_axis=0, concat_axis=0, tiled=True)]
    unnamed x1 -> x0, blocking collectives: 12.4 us -> none
    ppermute x0 -> x16, starting transfers between devices: none -> 9.48 us  [streamed(): move = lambda v, p: lax.ppermute(v, AXES, p)]
  transfers between devices with their start and end apart: 3 -> 17, of which waited for: 2 -> 5; matrix products, arithmetic and copies ran while one was open for 5% -> 9% of each run, Pallas kernels for 0% -> 35%
where the time goes in v1:
time: 150 us; the launch traced here: 148 us
  Pallas kernels  70 us (47%)
  waiting for transfers between devices  41.2 us (27%)
  starting transfers between devices  16.8 us (11%)
  other arithmetic  9.92 us (7%)
  local copies, waits for them, and re-layouts  7.61 us (5%)
  between operations  2.16 us (1%)
    pallas_call x4, Pallas kernels, level(): pl.pallas_call(functools.partial(level_kernel, order, first), out_shape=j...  70 us
    ppermute x16, waiting for transfers between devices, streamed(): move = lambda v, p: lax.ppermute(v, AXES, p)  26 us
    all_to_all x1, waiting for transfers between devices, streamed(): lax.all_to_all(parcels, ('z', 'y'), split_axis=0, concat_axis=0, tiled=True)  15.2 us
    ppermute x16, starting transfers between devices, streamed(): move = lambda v, p: lax.ppermute(v, AXES, p)  9.48 us
    all_to_all x1, starting transfers between devices, streamed(): lax.all_to_all(parcels, ('z', 'y'), split_axis=0, concat_axis=0, tiled=True)  7.31 us
    concatenate x1, other arithmetic, block_diagonal(): return jnp.concatenate(rows, axis=0)  6.48 us
  transfers between devices with their start and end apart: 17, of which 5 were waited for; matrix products, arithmetic and copies ran while one was open for 9% of the time, Pallas kernels for 35%

profile of v1, /device:TPU:0, one launch (start us, length us, event | category | flops | bytes accessed | tf_op | source)
XLA Modules:
  0.0 148.4 jit_solution(103754182773949388)
XLA Ops:
  0.0 0.7 convert_element_type.18
  0.7 1.0 copy.20
  1.8 0.8 pad_maximum_fusion.3
  2.7 1.0 pad_maximum_fusion.1
  3.7 7.3 %all-to-all-start = ((bf16[8,16,3968]{2,1,0:T(8,128)(2,1)}), bf16[8,16,3968]{2,1,0:T(8,128)(2,1)S(1)}, u32[]{:S(2)}, u32[]{:S(2)}) async-start(bf16[8,16,3968]{2,1,0:T(8,128)(2,1)} %pad_maximum_fusion.1), calls=%async_computation | async-start | bytes 2031616 | tf_op jit(solution)/shard_map/all_to_all | solution.py:157
  11.1 2.0 %collective-permute-start.13 = (bf16[2048,128]{1,0:T(8,128)(2,1)S(1)}, bf16[2048,128]{1,0:T(8,128)(2,1)S(1)}, u32[]{:S(2)}, u32[]{:S(2)}) collective-permute-start(bf16[2048,128]{1,0:T(8,128)(2,1)S(1)} %copy-done), channel_id=1, source_target_pairs={{0,2},{1,3},{2,0},{3,1},{4,6},{5,7},{6,4},{7,5},{8,10},{9,11},{10,... | collective-permute-start | bytes 1572872 | tf_op jit(solution)/shard_map/ppermute | solution.py:146
  13.1 1.5 collective-permute-start.1
  18.3 2.0 %copy.17 = bf16[4,224,224]{1,2,0:T(8,128)(2,1)} copy(bf16[4,224,224]{2,1,0:T(8,128)(2,1)} %param.13) | data formatting | bytes 802816 | tf_op args[3]
  20.5 1.7 %slice_bitcast_fusion.7 = (bf16[224,224]{1,0:T(8,128)(2,1)S(1)}, bf16[224,224]{1,0:T(8,128)(2,1)S(1)}, bf16[224,224]{1,0:T(8,128)(2,1)S(1)}, bf16[224,224]{1,0:T(8,128)(2,1)}) fusion(bf16[4,224,224]{2,1,0:T(8,128)(2,1)} %param.13), kind=kLoop, calls=%fused_computation.50 | loop fusion | bytes 802816 | tf_op jit(solution)/shard_map/squeeze | solution.py:117
  22.3 15.2 %all-to-all-done = bf16[8,16,3968]{2,1,0:T(8,128)(2,1)S(1)} async-done(((bf16[8,16,3968]{2,1,0:T(8,128)(2,1)}), bf16[8,16,3968]{2,1,0:T(8,128)(2,1)S(1)}, u32[]{:S(2)}, u32[]{:S(2)}) %all-to-all-start) | async-done | bytes 1015840 | tf_op jit(solution)/shard_map/all_to_all | solution.py:157
  37.8 0.8 copy-done.1
  38.5 8.8 %collective-permute-done.1.refs_4_ = bf16[2048,128]{1,0:T(8,128)(2,1)S(1)} collective-permute-done((bf16[2048,128]{1,0:T(8,128)(2,1)S(1)}, bf16[2048,128]{1,0:T(8,128)(2,1)S(1)}, u32[]{:S(2)}, u32[]{:S(2)}) %collective-permute-start.1) | collective-permute-done | bytes 524320 | tf_op jit(solution)/shard_map/ppermute | solution.py:146
  47.4 6.5 %fusion.15.refs_3_ = bf16[896,896]{1,0:T(8,128)(2,1)S(1)} fusion(bf16[224,224]{1,0:T(8,128)(2,1)S(1)} %get-tuple-element.11, bf16[224,224]{1,0:T(8,128)(2,1)S(1)} %get-tuple-element.12, bf16[224,224]{1,0:T(8,128)(2,1)S(1)} %get-tuple-element.13, bf16[224,224]{1,0:T(8,128)(2,1)S(1)} %get-tuple-element.10), kind=kLoop, calls=%fused_computation.21 | loop fusion | flops 16056320 | bytes 2007040 | tf_op jit(solution)/shard_map/concatenate | solution.py:119
  53.9 1.5 collective-permute-start.10
  55.4 5.4 %collective-permute-done.2.refs_4_ = bf16[2048,128]{1,0:T(8,128)(2,1)S(1)} collective-permute-done((bf16[2048,128]{1,0:T(8,128)(2,1)S(1)}, bf16[2048,128]{1,0:T(8,128)(2,1)S(1)}, u32[]{:S(2)}, u32[]{:S(2)}) %collective-permute-start.2) | collective-permute-done | bytes 524320 | tf_op jit(solution)/shard_map/ppermute | solution.py:146
  61.1 0.8 select_bitcast_fusion.2
  62.3 1.9 %collective-permute-start.7 = (bf16[2048,128]{1,0:T(8,128)(2,1)S(1)}, bf16[2048,128]{1,0:T(8,128)(2,1)S(1)}, u32[]{:S(2)}, u32[]{:S(2)}) collective-permute-start(bf16[2048,128]{1,0:T(8,128)(2,1)S(1)} %collective-permute-done.2.refs_4_), channel_id=1, source_target_pairs={{0,2},{1,3},{2,0},{3,1},{4,6},{5,7},{6,4},{7,5},{8,10},{9,11},{10,... | collective-permute-start | bytes 1572872 | tf_op jit(solution)/shard_map/ppermute | solution.py:146
  64.4 3.4 %collective-permute-done.10.refs_5_ = bf16[2048,128]{1,0:T(8,128)(2,1)S(1)} collective-permute-done((bf16[2048,128]{1,0:T(8,128)(2,1)S(1)}, bf16[2048,128]{1,0:T(8,128)(2,1)S(1)}, u32[]{:S(2)}, u32[]{:S(2)}) %collective-permute-start.10) | collective-permute-done | bytes 524320 | tf_op jit(solution)/shard_map/ppermute | solution.py:146
  67.7 8.3 %collective-permute-done.3.refs_4_ = bf16[2048,128]{1,0:T(8,128)(2,1)S(1)} collective-permute-done((bf16[2048,128]{1,0:T(8,128)(2,1)S(1)}, bf16[2048,128]{1,0:T(8,128)(2,1)S(1)}, u32[]{:S(2)}, u32[]{:S(2)}) %collective-permute-start.3) | collective-permute-done | bytes 524320 | tf_op jit(solution)/shard_map/ppermute | solution.py:146
  76.1 1.8 %collective-permute-start.4 = (bf16[2048,128]{1,0:T(8,128)(2,1)S(1)}, bf16[2048,128]{1,0:T(8,128)(2,1)S(1)}, u32[]{:S(2)}, u32[]{:S(2)}) collective-permute-start(bf16[2048,128]{1,0:T(8,128)(2,1)S(1)} %collective-permute-done.3.refs_4_), channel_id=1, source_target_pairs={{0,2},{1,3},{2,0},{3,1},{4,6},{5,7},{6,4},{7,5},{8,10},{9,11},{10,... | collective-permute-start | bytes 1572872 | tf_op jit(solution)/shard_map/ppermute | solution.py:146
  77.9 14.4 %level_first.1.refs_12_ = bf16[3,2048,896]{2,1,0:T(8,128)(2,1)} custom-call(s32[4]{0:T(128)S(1)} %pad_add_fusion.3.refs_0_, bf16[256,2048]{1,0:T(8,128)(2,1)S(1)} %fusion.21.refs_1_, bf16[3,256,896]{2,1,0:T(8,128)(2,1)S(1)} %pad_maximum_fusion.refs_2_, bf16[896,896]{1,0:T(8,128)(2,1)S(1)} %fusion.15.refs_3_, bf16[2048,128]{1,0:T(8,128)(2,1)S(1)} %copy-done, ...), custom_call_target="tpu_custom_call" | custom-call | flops 5637144576 | bytes 22020096 | tf_op jit(solution)/shard_map/level_first/pallas_call | solution.py:93
  92.9 18.4 %level_next.3.refs_12_ = bf16[3,2048,896]{2,1,0:T(8,128)(2,1)} custom-call(s32[4]{0:T(128)S(1)} %pad_add_fusion.2.refs_0_, bf16[256,2048]{1,0:T(8,128)(2,1)S(1)} %fusion.21.refs_1_, bf16[3,256,896]{2,1,0:T(8,128)(2,1)S(1)} %pad_maximum_fusion.refs_2_, bf16[896,896]{1,0:T(8,128)(2,1)S(1)} %fusion.15.refs_3_, ...), custom_call_target="tpu_custom_call", output_to_operand_aliasing={{}: (12, {})} | custom-call | flops 5637144576 | bytes 22020096 | tf_op jit(solution)/shard_map/level_next/pallas_call | solution.py:93
  111.3 18.7 %level_next.4.refs_12_ = bf16[3,2048,896]{2,1,0:T(8,128)(2,1)} custom-call(s32[4]{0:T(128)S(1)} %pad_add_fusion.1.refs_0_, bf16[256,2048]{1,0:T(8,128)(2,1)S(1)} %fusion.21.refs_1_, bf16[3,256,896]{2,1,0:T(8,128)(2,1)S(1)} %pad_maximum_fusion.refs_2_, bf16[896,896]{1,0:T(8,128)(2,1)S(1)} %fusion.15.refs_3_, ...), custom_call_target="tpu_custom_call", output_to_operand_aliasing={{}: (12, {})} | custom-call | flops 5637144576 | bytes 22020096 | tf_op jit(solution)/shard_map/level_next/pallas_call | solution.py:93
  130.0 18.4 %level_next.5 = bf16[3,2048,896]{2,1,0:T(8,128)(2,1)} custom-call(s32[4]{0:T(128)S(1)} %pad_add_fusion.refs_0_, bf16[256,2048]{1,0:T(8,128)(2,1)S(1)} %fusion.21.refs_1_, bf16[3,256,896]{2,1,0:T(8,128)(2,1)S(1)} %pad_maximum_fusion.refs_2_, bf16[896,896]{1,0:T(8,128)(2,1)S(1)} %fusion.15.refs_3_, ...), custom_call_target="tpu_custom_call", output_to_operand_aliasing={{}: (12, {})} | custom-call | flops 5637144576 | bytes 22020096 | tf_op jit(solution)/shard_map/level_next/pallas_call | solution.py:93
  (57 shorter events, 3.9 us)
Async XLA Ops:
  2.7 8.4 %copy-start = (bf16[2048,128]{1,0:T(8,128)(2,1)S(1)}, bf16[2048,128]{1,0:T(8,128)(2,1)}, u32[]{:S(2)}) copy-start(bf16[2048,128]{1,0:T(8,128)(2,1)} %refs_4_.1) | copy-start | bytes 1572868
  2.7 11.9 %copy-start.5 = (s32[4]{0:T(128)S(1)}, s32[4]{0:T(128)}, u32[]{:S(2)}) copy-start(s32[4]{0:T(128)} %constant.40.clone) | copy-start | bytes 52
  2.7 13.1 %copy-start.4 = (s32[4]{0:T(128)S(1)}, s32[4]{0:T(128)}, u32[]{:S(2)}) copy-start(s32[4]{0:T(128)} %constant.41.clone) | copy-start | bytes 52
  2.7 14.3 %copy-start.3 = (s32[4]{0:T(128)S(1)}, s32[4]{0:T(128)}, u32[]{:S(2)}) copy-start(s32[4]{0:T(128)} %constant.42.clone) | copy-start | bytes 52
  3.7 33.7 %all-to-all-start = ((bf16[8,16,3968]{2,1,0:T(8,128)(2,1)}), bf16[8,16,3968]{2,1,0:T(8,128)(2,1)S(1)}, u32[]{:S(2)}, u32[]{:S(2)}) async-start(bf16[8,16,3968]{2,1,0:T(8,128)(2,1)} %pad_maximum_fusion.1), calls=%async_computation | async-start | bytes 2031616 | tf_op jit(solution)/shard_map/all_to_all | solution.py:157
  11.1 44.3 %collective-permute-start.13 = (bf16[2048,128]{1,0:T(8,128)(2,1)S(1)}, bf16[2048,128]{1,0:T(8,128)(2,1)S(1)}, u32[]{:S(2)}, u32[]{:S(2)}) collective-permute-start(bf16[2048,128]{1,0:T(8,128)(2,1)S(1)} %copy-done), channel_id=1, source_target_pairs={{0,2},{1,3},{2,0},{3,1},{4,6},{5,7},{6,4},{7,5},{8,10},{9,11},{10,... | collective-permute-start | bytes 1572872 | tf_op jit(solution)/shard_map/ppermute | solution.py:146
  13.1 49.2 %collective-permute-start.14 = (bf16[2048,128]{1,0:T(8,128)(2,1)S(1)}, bf16[2048,128]{1,0:T(8,128)(2,1)S(1)}, u32[]{:S(2)}, u32[]{:S(2)}) collective-permute-start(bf16[2048,128]{1,0:T(8,128)(2,1)S(1)} %copy-done), channel_id=1, source_target_pairs={{0,1},{1,0},{2,3},{3,2},{4,5},{5,4},{6,7},{7,6},{8,9},{9,8},{10,11... | collective-permute-start | bytes 1572872 | tf_op jit(solution)/shard_map/ppermute | solution.py:146
  13.1 34.3 %collective-permute-start.1 = (bf16[2048,128]{1,0:T(8,128)(2,1)S(1)}, bf16[2048,128]{1,0:T(8,128)(2,1)S(1)}, u32[]{:S(2)}, u32[]{:S(2)}) collective-permute-start(bf16[2048,128]{1,0:T(8,128)(2,1)S(1)} %copy-done), channel_id=1, source_target_pairs={{0,4},{1,5},{2,6},{3,7},{4,12},{5,13},{6,14},{7,15},{8,0},{9,1},{1... | collective-permute-start | bytes 1572872 | tf_op jit(solution)/shard_map/ppermute | solution.py:146
  37.7 23.2 %collective-permute-start = (bf16[128,3072]{1,0:T(8,128)(2,1)S(1)}, bf16[128,3072]{1,0:T(8,128)(2,1)S(1)}, u32[]{:S(2)}, u32[]{:S(2)}) collective-permute-start(bf16[128,3072]{1,0:T(8,128)(2,1)S(1)} %pad_maximum_fusion.2), channel_id=1, source_target_pairs={{0,1},{1,0},{2,3},{3,2},{4,5},{5,4},{6,7},{7,6},{8,9},{9,8},{10,11... | collective-permute-start | bytes 2359304 | tf_op jit(solution)/shard_map/ppermute | solution.py:146
  47.4 13.5 %collective-permute-start.2 = (bf16[2048,128]{1,0:T(8,128)(2,1)S(1)}, bf16[2048,128]{1,0:T(8,128)(2,1)S(1)}, u32[]{:S(2)}, u32[]{:S(2)}) collective-permute-start(bf16[2048,128]{1,0:T(8,128)(2,1)S(1)} %collective-permute-done.1.refs_4_), channel_id=1, source_target_pairs={{0,4},{1,5},{2,6},{3,7},{4,12},{5,13},{6,14},{7,15},{8,0},{9,1},{1... | collective-permute-start | bytes 1572872 | tf_op jit(solution)/shard_map/ppermute | solution.py:146
  47.4 13.7 %copy-start.2 = (bf16[224,224]{1,0:T(8,128)(2,1)S(1)}, bf16[224,224]{1,0:T(8,128)(2,1)}, u32[]{:S(2)}) copy-start(bf16[224,224]{1,0:T(8,128)(2,1)} %get-tuple-element.20) | copy-start | bytes 301060
  53.9 13.8 %collective-permute-start.10 = (bf16[2048,128]{1,0:T(8,128)(2,1)S(1)}, bf16[2048,128]{1,0:T(8,128)(2,1)S(1)}, u32[]{:S(2)}, u32[]{:S(2)}) collective-permute-start(bf16[2048,128]{1,0:T(8,128)(2,1)S(1)} %collective-permute-done.1.refs_4_), channel_id=1, source_target_pairs={{0,2},{1,3},{2,0},{3,1},{4,6},{5,7},{6,4},{7,5},{8,10},{9,11},{10,... | collective-permute-start | bytes 1572872 | tf_op jit(solution)/shard_map/ppermute | solution.py:146
  55.4 36.9 %collective-permute-start.11 = (bf16[2048,128]{1,0:T(8,128)(2,1)S(1)}, bf16[2048,128]{1,0:T(8,128)(2,1)S(1)}, u32[]{:S(2)}, u32[]{:S(2)}) collective-permute-start(bf16[2048,128]{1,0:T(8,128)(2,1)S(1)} %collective-permute-done.1.refs_4_), channel_id=1, source_target_pairs={{0,1},{1,0},{2,3},{3,2},{4,5},{5,4},{6,7},{7,6},{8,9},{9,8},{10,11... | collective-permute-start | bytes 1572872 | tf_op jit(solution)/shard_map/ppermute | solution.py:146
  60.8 3.3 %collective-permute-start.15 = (bf16[2048,128]{1,0:T(8,128)(2,1)S(1)}, bf16[2048,128]{1,0:T(8,128)(2,1)S(1)}, u32[]{:S(2)}, u32[]{:S(2)}) collective-permute-start(bf16[2048,128]{1,0:T(8,128)(2,1)S(1)} %collective-permute-done.13.refs_5_), channel_id=1, source_target_pairs={{0,1},{1,0},{2,3},{3,2},{4,5},{5,4},{6,7},{7,6},{8,9},{9,8},{10,11... | collective-permute-start | bytes 1572872 | tf_op jit(solution)/shard_map/ppermute | solution.py:146
  60.8 15.2 %collective-permute-start.3 = (bf16[2048,128]{1,0:T(8,128)(2,1)S(1)}, bf16[2048,128]{1,0:T(8,128)(2,1)S(1)}, u32[]{:S(2)}, u32[]{:S(2)}) collective-permute-start(bf16[2048,128]{1,0:T(8,128)(2,1)S(1)} %collective-permute-done.2.refs_4_), channel_id=1, source_target_pairs={{0,4},{1,5},{2,6},{3,7},{4,12},{5,13},{6,14},{7,15},{8,0},{9,1},{1... | collective-permute-start | bytes 1572872 | tf_op jit(solution)/shard_map/ppermute | solution.py:146
  61.1 16.7 %slice-start = ((s8[7340032]{0:T(1024)(128)(4,1)}), s8[4194304]{0:T(1024)(128)(4,1)S(1)}, s32[]{:S(2)}) async-start(s8[7340032]{0:T(1024)(128)(4,1)} %bitcast.50), calls=%async_computation.1 | async-start | bytes 8388608
  61.1 16.7 %slice-start.1 = ((s8[7340032]{0:T(1024)(128)(4,1)}), s8[3145728]{0:T(1024)(128)(4,1)S(1)}, s32[]{:S(2)}) async-start(s8[7340032]{0:T(1024)(128)(4,1)} %bitcast.50), calls=%async_computation.2 | async-start | bytes 6291456
  62.3 30.0 %collective-permute-start.7 = (bf16[2048,128]{1,0:T(8,128)(2,1)S(1)}, bf16[2048,128]{1,0:T(8,128)(2,1)S(1)}, u32[]{:S(2)}, u32[]{:S(2)}) collective-permute-start(bf16[2048,128]{1,0:T(8,128)(2,1)S(1)} %collective-permute-done.2.refs_4_), channel_id=1, source_target_pairs={{0,2},{1,3},{2,0},{3,1},{4,6},{5,7},{6,4},{7,5},{8,10},{9,11},{10,... | collective-permute-start | bytes 1572872 | tf_op jit(solution)/shard_map/ppermute | solution.py:146
  64.1 47.2 %collective-permute-start.8 = (bf16[2048,128]{1,0:T(8,128)(2,1)S(1)}, bf16[2048,128]{1,0:T(8,128)(2,1)S(1)}, u32[]{:S(2)}, u32[]{:S(2)}) collective-permute-start(bf16[2048,128]{1,0:T(8,128)(2,1)S(1)} %collective-permute-done.2.refs_4_), channel_id=1, source_target_pairs={{0,1},{1,0},{2,3},{3,2},{4,5},{5,4},{6,7},{7,6},{8,9},{9,8},{10,11... | collective-permute-start | bytes 1572872 | tf_op jit(solution)/shard_map/ppermute | solution.py:146
  67.7 25.1 %collective-permute-start.12 = (bf16[2048,128]{1,0:T(8,128)(2,1)S(1)}, bf16[2048,128]{1,0:T(8,128)(2,1)S(1)}, u32[]{:S(2)}, u32[]{:S(2)}) collective-permute-start(bf16[2048,128]{1,0:T(8,128)(2,1)S(1)} %collective-permute-done.10.refs_5_), channel_id=1, source_target_pairs={{0,1},{1,0},{2,3},{3,2},{4,5},{5,4},{6,7},{7,6},{8,9},{9,8},{10,11... | collective-permute-start | bytes 1572872 | tf_op jit(solution)/shard_map/ppermute | solution.py:146
  76.1 16.7 %collective-permute-start.4 = (bf16[2048,128]{1,0:T(8,128)(2,1)S(1)}, bf16[2048,128]{1,0:T(8,128)(2,1)S(1)}, u32[]{:S(2)}, u32[]{:S(2)}) collective-permute-start(bf16[2048,128]{1,0:T(8,128)(2,1)S(1)} %collective-permute-done.3.refs_4_), channel_id=1, source_target_pairs={{0,2},{1,3},{2,0},{3,1},{4,6},{5,7},{6,4},{7,5},{8,10},{9,11},{10,... | collective-permute-start | bytes 1572872 | tf_op jit(solution)/shard_map/ppermute | solution.py:146
  92.3 37.7 %collective-permute-start.5 = (bf16[2048,128]{1,0:T(8,128)(2,1)S(1)}, bf16[2048,128]{1,0:T(8,128)(2,1)S(1)}, u32[]{:S(2)}, u32[]{:S(2)}) collective-permute-start(bf16[2048,128]{1,0:T(8,128)(2,1)S(1)} %collective-permute-done.3.refs_4_), channel_id=1, source_target_pairs={{0,1},{1,0},{2,3},{3,2},{4,5},{5,4},{6,7},{7,6},{8,9},{9,8},{10,11... | collective-permute-start | bytes 1572872 | tf_op jit(solution)/shard_map/ppermute | solution.py:146
  92.3 19.0 %collective-permute-start.9 = (bf16[2048,128]{1,0:T(8,128)(2,1)S(1)}, bf16[2048,128]{1,0:T(8,128)(2,1)S(1)}, u32[]{:S(2)}, u32[]{:S(2)}) collective-permute-start(bf16[2048,128]{1,0:T(8,128)(2,1)S(1)} %collective-permute-done.7.refs_5_), channel_id=1, source_target_pairs={{0,1},{1,0},{2,3},{3,2},{4,5},{5,4},{6,7},{7,6},{8,9},{9,8},{10,11... | collective-permute-start | bytes 1572872 | tf_op jit(solution)/shard_map/ppermute | solution.py:146
  92.8 37.2 %collective-permute-start.6 = (bf16[2048,128]{1,0:T(8,128)(2,1)S(1)}, bf16[2048,128]{1,0:T(8,128)(2,1)S(1)}, u32[]{:S(2)}, u32[]{:S(2)}) collective-permute-start(bf16[2048,128]{1,0:T(8,128)(2,1)S(1)} %collective-permute-done.4.refs_5_), channel_id=1, source_target_pairs={{0,1},{1,0},{2,3},{3,2},{4,5},{5,4},{6,7},{7,6},{8,9},{9,8},{10,11... | collective-permute-start | bytes 1572872 | tf_op jit(solution)/shard_map/ppermute | solution.py:146
  (1 other events, 1.0 us)

commit v2 on v1

v2 whole, which is shorter than its diff:
```python
import functools

import jax
import jax.numpy as jnp
from jax import lax
from jax.experimental import pallas as pl
from jax.experimental.pallas import tpu as pltpu
from jax.sharding import Mesh
from jax.sharding import PartitionSpec as P


QUERIES = 3
LANES = 128
ROWS = 256
AXES = ("g", "z", "y", "c")


def windows(width, order):
    out = []
    for n0 in range(0, width, 2 * LANES):
        n1 = min(n0 + 2 * LANES, width)
        k0 = (n0 // order) * order // LANES * LANES
        k1 = min(width, -(-((n1 - 1) // order + 1) * order // LANES) * LANES)
        out.append((n0, n1, k0, k1))
    return out


def basis_kernel(blocks_ref, dense_ref):
    count, order, _ = blocks_ref.shape
    dense_ref[...] = jnp.zeros_like(dense_ref)
    for b in range(count):
        dense_ref[b * order : (b + 1) * order, b * order : (b + 1) * order] = blocks_ref[b]


def block_diagonal(blocks):
    count, order, _ = blocks.shape
    return pl.pallas_call(
        basis_kernel,
        out_shape=jax.ShapeDtypeStruct((count * order,) * 2, blocks.dtype),
        compiler_params=pltpu.CompilerParams(vmem_limit_bytes=8 << 20),
        name="dense_basis",
    )(blocks)


def tokens_kernel(order, core_ref, got_ref, swap_ref, dense_ref, sel_ref, og_ref):
    half = got_ref.shape[0]
    units = og_ref.shape[1]
    width = dense_ref.shape[0]
    shared = got_ref.shape[1] - units - LANES
    at = pl.ds(pl.multiple_of(core_ref[0] * width, LANES), width)
    for i, ref in enumerate((got_ref, swap_ref)):
        rows = slice(i * half, (i + 1) * half)
        og_ref[rows, :] = ref[:, shared : shared + units]
        ids = ref[:, shared + units :][:, :1].astype(jnp.float32)
        columns = ref[:, at]
        for n0, n1, k0, k1 in windows(width, order):
            turned = jnp.dot(
                columns[:, k0:k1], dense_ref[k0:k1, n0:n1], preferred_element_type=jnp.float32
            )
            for q in range(QUERIES):
                sel_ref[q, rows, n0:n1] = jnp.where(ids == float(q), turned, 0.0).astype(
                    jnp.bfloat16
                )


def tokens_of(order, core, got, swapped, dense, units):
    half = got.shape[0]
    width = dense.shape[0]
    return pl.pallas_call(
        functools.partial(tokens_kernel, order),
        out_shape=(
            jax.ShapeDtypeStruct((QUERIES, 2 * half, width), jnp.bfloat16),
            jax.ShapeDtypeStruct((2 * half, units), jnp.bfloat16),
        ),
        in_specs=[
            pl.BlockSpec(memory_space=pltpu.SMEM),
            pl.BlockSpec(got.shape, lambda: (0, 0)),
            pl.BlockSpec(swapped.shape, lambda: (0, 0)),
            pl.BlockSpec(dense.shape, lambda: (0, 0)),
        ],
        out_specs=(
            pl.BlockSpec((QUERIES, 2 * half, width), lambda: (0, 0, 0)),
            pl.BlockSpec((2 * half, units), lambda: (0, 0)),
        ),
        compiler_params=pltpu.CompilerParams(vmem_limit_bytes=20 << 20),
        cost_estimate=pl.CostEstimate(
            flops=4 * half * width * width, bytes_accessed=4 << 20, transcendentals=0
        ),
        name="tokens",
    )(core, got, swapped, dense)


def half_kernel(order, first, count, *refs):
    ids_ref, og_ref, sel_ref, dense_ref = refs[:4]
    basis_refs = refs[4 : 4 + count]
    eig_ref = refs[4 + count]
    if first:
        acc_ref = None
        out_ref, rgt_ref, inv_ref, rb_ref, sems = refs[5 + count :]
    else:
        acc_ref, out_ref, rgt_ref, inv_ref, rb_ref, sems = refs[5 + count :]
    step = pl.program_id(0)
    rows, width = out_ref.shape[1:]
    shard = basis_refs[0].shape[1]

    @pl.when(step == 0)
    def _():
        def fetch(j):
            at = pl.ds(pl.multiple_of(ids_ref[j] * shard, shard), shard)
            to = pl.ds(pl.multiple_of(j * shard, shard), shard)
            return pltpu.make_async_copy(eig_ref.at[at, :], inv_ref.at[to, :], sems.at[j])

        for j in range(count):
            fetch(j).start()
        for j in range(0, count, 2):
            basis = jnp.concatenate([r[...] for r in basis_refs[j : j + 2]], axis=1)
            rg = jnp.dot(og_ref[...], basis, preferred_element_type=jnp.float32)
            rgt_ref[j * shard : (j + 2) * shard, :] = rg.astype(jnp.bfloat16).T

        @pl.loop(0, count // 2)
        def _(i):
            fetch(2 * i).wait()
            fetch(2 * i + 1).wait()
            at = pl.ds(pl.multiple_of(i * 2 * shard, 2 * shard), 2 * shard)
            inv = 1.0 / inv_ref[at, :]
            for q in range(QUERIES):
                m = jnp.dot(rgt_ref[at, :], sel_ref[q], preferred_element_type=jnp.float32)
                s = (m * inv).astype(jnp.bfloat16)
                for n0, n1, k0, k1 in windows(width, order):
                    back = lax.dot_general(
                        s[:, k0:k1],
                        dense_ref[n0:n1, k0:k1],
                        (((1,), (1,)), ((), ())),
                        preferred_element_type=jnp.float32,
                    )
                    rb_ref[at, q * width + n0 : q * width + n1] = back.astype(jnp.bfloat16)

    at = pl.ds(pl.multiple_of(step * rows, rows), rows)
    lhs = jnp.concatenate([r[at, :] for r in basis_refs], axis=1)
    part = jnp.dot(lhs, rb_ref[...], preferred_element_type=jnp.float32)
    for q in range(QUERIES):
        own = part[:, q * width : (q + 1) * width]
        if not first:
            own = own + acc_ref[q].astype(jnp.float32)
        out_ref[q] = own.astype(out_ref.dtype)


def half_of(order, shard_ids, og, sel, dense, bases, eig, acc):
    tokens, units = og.shape
    width = sel.shape[2]
    shard = bases[0].shape[1]
    count = len(bases)
    rows = min(units, ROWS)
    first = acc is None
    whole = pl.BlockSpec(memory_space=pltpu.VMEM)
    once = pl.Buffered(1)
    in_specs = [
        pl.BlockSpec(og.shape, lambda i, s: (0, 0), pipeline_mode=once),
        pl.BlockSpec(sel.shape, lambda i, s: (0, 0, 0), pipeline_mode=once),
        pl.BlockSpec(dense.shape, lambda i, s: (0, 0), pipeline_mode=once),
    ]
    in_specs += [whole] * count
    in_specs.append(pl.BlockSpec(memory_space=pltpu.HBM))
    out_block = pl.BlockSpec((QUERIES, rows, width), lambda i, s: (0, i, 0))
    args = [og, sel, dense, *bases, pltpu.with_memory_space_constraint(eig, pltpu.HBM)]
    if not first:
        in_specs.append(out_block)
        args.append(pltpu.with_memory_space_constraint(acc, pltpu.HBM))
    return pl.pallas_call(
        functools.partial(half_kernel, order, first, count),
        out_shape=pltpu.HBM((QUERIES, units, width), jnp.bfloat16),
        grid_spec=pltpu.PrefetchScalarGridSpec(
            num_scalar_prefetch=1,
            grid=(units // rows,),
            in_specs=in_specs,
            out_specs=out_block,
            scratch_shapes=[
                pltpu.VMEM((count * shard, tokens), jnp.bfloat16),
                pltpu.VMEM((count * shard, width), jnp.float32),
                pltpu.VMEM((count * shard, QUERIES * width), jnp.bfloat16),
                pltpu.SemaphoreType.DMA((count,)),
            ],
        ),
        compiler_params=pltpu.CompilerParams(
            dimension_semantics=("arbitrary",), vmem_limit_bytes=30 << 20
        ),
        cost_estimate=pl.CostEstimate(
            flops=2 * QUERIES * width * count * shard * units,
            bytes_accessed=QUERIES * units * width * (2 if first else 4),
            transcendentals=0,
        ),
        name="half_first" if first else "half_next",
    )(shard_ids, *args)


def ring_of(nz):
    return [0] + list(range(1, nz, 2)) + [z for z in range(nz - 1, 0, -1) if z % 2 == 0]


def streamed(shape, activations, out_grads, query_ids, act_basis, grad_basis, eigenvalues):
    ng, nz, ny, nc = shape
    count, order, _ = act_basis.shape
    width = count * order
    tokens = activations.shape[0]
    chips = nz * ny
    units = grad_basis.shape[0]

    def enc(g, z, y, c):
        return ((g * nz + z) * ny + y) * nc + c

    every = [
        (g, z, y, c) for g in range(ng) for z in range(nz) for y in range(ny) for c in range(nc)
    ]
    order_z = ring_of(nz)
    follow = {z: order_z[(i + 1) % nz] for i, z in enumerate(order_z)}
    before = {v: k for k, v in follow.items()}
    perm_core = [(enc(g, z, y, c), enc(g, z, y, 1 - c)) for g, z, y, c in every]
    perm_y = [(enc(g, z, y, c), enc(g, z, 1 - y, c)) for g, z, y, c in every]
    perm_z = [(enc(g, z, y, c), enc(g, follow[z], y, c)) for g, z, y, c in every]
    perm_zr = [(t, s) for s, t in perm_z]
    move = lambda v, p: lax.ppermute(v, AXES, p)

    ids = jnp.broadcast_to(query_ids.astype(jnp.bfloat16)[:, None], (tokens, LANES))
    common = jnp.concatenate([out_grads, ids], axis=1)
    parcels = jnp.concatenate(
        [
            activations.reshape(tokens, chips, nc * width).transpose(1, 0, 2),
            jnp.broadcast_to(common[None], (chips,) + common.shape),
        ],
        axis=2,
    )
    got = lax.all_to_all(parcels, ("z", "y"), split_axis=0, concat_axis=0, tiled=True)
    got = got.reshape(chips * tokens, nc * width + units + LANES)
    swapped = move(got, perm_core)

    along = [grad_basis] + [None] * (nz - 1)
    for k in range(1, nz // 2 + 1):
        along[k] = move(along[k - 1], perm_z)
        if nz - k > k:
            along[nz - k] = move(along[(nz - k + 1) % nz], perm_zr)
    levels = []
    for k in range(nz):
        across = move(along[k], perm_y)
        far = move(along[k], perm_core)
        far_across = move(across, perm_core)
        levels.append((along[k], across, far, far_across))

    z, y, c = lax.axis_index("z"), lax.axis_index("y"), lax.axis_index("c")
    dense = block_diagonal(act_basis)
    sel, og = tokens_of(
        order, c.astype(jnp.int32)[None], got, swapped, dense, units
    )

    ids_at, level_z = [], list(range(nz))
    for _ in range(nz):
        zk = sum(jnp.where(z == i, v, 0) for i, v in enumerate(level_z))
        ids_at.append([(zk * ny + yy) * nc + cc for cc in (c, 1 - c) for yy in (y, 1 - y)])
        level_z = [before[v] for v in level_z]
    acc = None
    for k in range(0, nz, nz // 2):
        span = range(k, k + nz // 2)
        shard_ids = jnp.stack([i for j in span for i in ids_at[j]]).astype(jnp.int32)
        bases = [b for j in span for b in levels[j]]
        acc = half_of(order, shard_ids, og, sel, dense, bases, eigenvalues, acc)
    return acc


def plain(activations, out_grads, query_ids, act_basis, grad_basis, eigenvalues):
    local_blocks, block_order = act_basis.shape[:2]
    out_units = grad_basis.shape[0]
    columns = lax.all_to_all(activations, AXES[1:], split_axis=1, concat_axis=0, tiled=True)
    all_tokens = columns.shape[0]
    local_width = local_blocks * block_order
    rotated_act = jnp.einsum(
        "tbi,bik->tbk",
        columns.reshape(all_tokens, local_blocks, block_order),
        act_basis,
        preferred_element_type=jnp.float32,
    )
    rotated_act = rotated_act.astype(jnp.bfloat16).reshape(all_tokens, local_width)
    full_basis = lax.all_gather(grad_basis, AXES[1:], axis=1, tiled=True)
    own_rotated = jnp.dot(out_grads, full_basis, preferred_element_type=jnp.float32).astype(
        jnp.bfloat16
    )
    rotated_grad = lax.all_gather(own_rotated, AXES[1:], axis=0, tiled=True)
    token_query = lax.all_gather(query_ids, AXES[1:], axis=0, tiled=True)
    selector = (token_query[:, None] == jnp.arange(QUERIES, dtype=jnp.int32)[None, :]).astype(
        jnp.bfloat16
    )
    results = []
    for q in range(QUERIES):
        moments = lax.dot_general(
            rotated_grad,
            rotated_act * selector[:, q : q + 1],
            (((0,), (0,)), ((), ())),
            preferred_element_type=jnp.float32,
        )
        scaled = (moments / eigenvalues).astype(jnp.bfloat16)
        back = jnp.einsum(
            "dbk,bik->dbi",
            scaled.reshape(out_units, local_blocks, block_order),
            act_basis,
            preferred_element_type=jnp.float32,
        )
        back = back.astype(jnp.bfloat16).reshape(out_units, local_width)
        results.append(
            jnp.dot(full_basis, back, preferred_element_type=jnp.float32).astype(jnp.bfloat16)
        )
    return jnp.stack(results, axis=0)


def solution(mesh):
    ng, ns = mesh.shape["groups"], mesh.shape["seq"]
    ny = nc = 2
    nz = ns // (ny * nc)
    shape = (ng, nz, ny, nc)
    fine = Mesh(mesh.devices.reshape(shape), AXES)
    seq = AXES[1:]

    def body(activations, out_grads, query_ids, act_basis, grad_basis, eigenvalues):
        shard = grad_basis.shape[1]
        width = act_basis.shape[0] * act_basis.shape[1]
        if shard % LANES or width % LANES or nz % 2:
            return plain(activations, out_grads, query_ids, act_basis, grad_basis, eigenvalues)
        return streamed(
            shape, activations, out_grads, query_ids, act_basis, grad_basis, eigenvalues
        )

    return jax.shard_map(
        body,
        mesh=fine,
        in_specs=(
            P(AXES, None),
            P(AXES, None),
            P(AXES),
            P(seq, None, None),
            P(None, seq),
            P(None, seq),
        ),
        out_specs=P("g", None, seq),
        check_vma=False,
    )
```

time: 150 us -> 148 us (0.987)
  waiting for transfers between devices: 41.2 us -> 70.7 us
  Pallas kernels: 70 us -> 51.3 us
  other arithmetic: 9.92 us -> 2.53 us
  between operations: 2.16 us -> 0.13 us
    ppermute x16, waiting for transfers between devices: 26 us -> 47.8 us  [streamed(): move = lambda v, p: lax.ppermute(v, AXES, p)]
    pallas_call x4, Pallas kernels: 70 us -> 51.3 us  [the longest x2 50.6 us: half_of(): pl.pallas_call(functools.partial(half_kernel, order, first, count), out_s...]
    all_to_all x1, waiting for transfers between devices: 15.2 us -> 22.9 us  [streamed(): lax.all_to_all(parcels, ('z', 'y'), split_axis=0, concat_axis=0, tiled=True)]
    concatenate x3 -> x0, other arithmetic: 6.67 us -> none  [the longest x1 6.48 us: block_diagonal(): return jnp.concatenate(rows, axis=0)]
    unnamed x17 -> x14, local copies, waits for them, and re-layouts: 2.8 us -> 5.06 us
    dynamic_slice x3 -> x0, local copies, waits for them, and re-layouts: 1.79 us -> none  [streamed(): zk = jnp.asarray(level_z, jnp.int32)[z]]
    squeeze x2 -> x0, local copies, waits for them, and re-layouts: 1.76 us -> none  [block_diagonal(): blocks[b]]
  transfers between devices with their start and end apart: 17 -> 17, of which waited for: 5 -> 6; matrix products, arithmetic and copies ran while one was open for 9% -> 0% of each run, Pallas kernels for 35% -> 18%
where the time goes in v2:
time: 148 us; the launch traced here: 147 us
  waiting for transfers between devices  70.7 us (48%)
  Pallas kernels  51.3 us (35%)
  starting transfers between devices  15.7 us (11%)
  local copies, waits for them, and re-layouts  6.4 us (4%)
  other arithmetic  2.53 us (2%)
    pallas_call x2, Pallas kernels, half_of(): pl.pallas_call(functools.partial(half_kernel, order, first, count), out_s...  50.6 us
    ppermute x16, waiting for transfers between devices, streamed(): move = lambda v, p: lax.ppermute(v, AXES, p)  47.8 us
    all_to_all x1, waiting for transfers between devices, streamed(): lax.all_to_all(parcels, ('z', 'y'), split_axis=0, concat_axis=0, tiled=True)  22.9 us
    ppermute x16, starting transfers between devices, streamed(): move = lambda v, p: lax.ppermute(v, AXES, p)  8.43 us
    all_to_all x1, starting transfers between devices, streamed(): lax.all_to_all(parcels, ('z', 'y'), split_axis=0, concat_axis=0, tiled=True)  7.31 us
    unnamed x14, local copies, waits for them, and re-layouts  5.06 us
  transfers between devices with their start and end apart: 17, of which 6 were waited for; matrix products, arithmetic and copies ran while one was open for 0% of the time, Pallas kernels for 18%

profile of v2, /device:TPU:0, one launch (start us, length us, event | category | flops | bytes accessed | tf_op | source)
XLA Modules:
  0.0 146.8 jit_solution(352960065262402904)
XLA Ops:
  0.0 0.7 convert_element_type.3
  0.7 1.0 copy.10
  1.8 0.8 pad_maximum_fusion.1
  2.7 1.0 pad_maximum_fusion
  3.7 7.3 %all-to-all-start = ((bf16[8,16,3968]{2,1,0:T(8,128)(2,1)}), bf16[8,16,3968]{2,1,0:T(8,128)(2,1)S(1)}, u32[]{:S(2)}, u32[]{:S(2)}) async-start(bf16[8,16,3968]{2,1,0:T(8,128)(2,1)} %pad_maximum_fusion), calls=%async_computation | async-start | bytes 2031616 | tf_op jit(solution)/shard_map/all_to_all | solution.py:232
  11.0 2.0 %collective-permute-start.1 = (bf16[2048,128]{1,0:T(8,128)(2,1)S(1)}, bf16[2048,128]{1,0:T(8,128)(2,1)}, u32[]{:S(2)}, u32[]{:S(2)}) collective-permute-start(bf16[2048,128]{1,0:T(8,128)(2,1)S(1)} %copy-done.3), channel_id=1, source_target_pairs={{0,4},{1,5},{2,6},{3,7},{4,12},{5,13},{6,14},{7,15},{8,0},{9,1},{1... | collective-permute-start | bytes 1572872 | tf_op jit(solution)/shard_map/ppermute | solution.py:221
  13.1 1.5 collective-permute-start.10
  14.5 22.9 %all-to-all-done = bf16[8,16,3968]{2,1,0:T(8,128)(2,1)S(1)} async-done(((bf16[8,16,3968]{2,1,0:T(8,128)(2,1)}), bf16[8,16,3968]{2,1,0:T(8,128)(2,1)S(1)}, u32[]{:S(2)}, u32[]{:S(2)}) %all-to-all-start) | async-done | bytes 1015840 | tf_op jit(solution)/shard_map/all_to_all | solution.py:232
  37.5 0.5 collective-permute-start.11
  38.0 20.7 %collective-permute-done.1.refs_8_ = bf16[2048,128]{1,0:T(8,128)(2,1)} collective-permute-done((bf16[2048,128]{1,0:T(8,128)(2,1)S(1)}, bf16[2048,128]{1,0:T(8,128)(2,1)}, u32[]{:S(2)}, u32[]{:S(2)}) %collective-permute-start.1) | collective-permute-done | bytes 524320 | tf_op jit(solution)/shard_map/ppermute | solution.py:221
  58.7 1.4 collective-permute-start.13
  60.2 0.8 copy-done.5
  61.0 0.6 collective-permute-start.7
  61.6 12.2 %collective-permute-done.13.refs_9_ = bf16[2048,128]{1,0:T(8,128)(2,1)} collective-permute-done((bf16[2048,128]{1,0:T(8,128)(2,1)}, bf16[2048,128]{1,0:T(8,128)(2,1)}, u32[]{:S(2)}, u32[]{:S(2)}) %collective-permute-start.13) | collective-permute-done | bytes 524320 | tf_op jit(solution)/shard_map/ppermute | solution.py:221
  74.0 1.2 collective-permute-start.3
  75.2 1.0 copy-done
  76.8 1.2 copy-done.1
  78.9 6.2 %collective-permute-done.7.refs_9_ = bf16[2048,128]{1,0:T(8,128)(2,1)} collective-permute-done((bf16[2048,128]{1,0:T(8,128)(2,1)}, bf16[2048,128]{1,0:T(8,128)(2,1)}, u32[]{:S(2)}, u32[]{:S(2)}) %collective-permute-start.7) | collective-permute-done | bytes 524320 | tf_op jit(solution)/shard_map/ppermute | solution.py:221
  85.0 0.5 collective-permute-start.9
  85.5 8.5 %collective-permute-done.3.refs_5_ = bf16[2048,128]{1,0:T(8,128)(2,1)} collective-permute-done((bf16[2048,128]{1,0:T(8,128)(2,1)}, bf16[2048,128]{1,0:T(8,128)(2,1)}, u32[]{:S(2)}, u32[]{:S(2)}) %collective-permute-start.3) | collective-permute-done | bytes 524320 | tf_op jit(solution)/shard_map/ppermute | solution.py:221
  94.1 1.0 copy-done.4
  95.1 1.0 copy-done.6
  96.2 25.1 %half_first.1.refs_13_ = bf16[3,2048,896]{2,1,0:T(8,128)(2,1)} custom-call(s32[8]{0:T(128)S(1)} %stack.71.refs_0_, bf16[256,2048]{1,0:T(8,128)(2,1)S(1)} %get-tuple-element.7.refs_1_, bf16[3,256,896]{2,1,0:T(8,128)(2,1)S(1)} %get-tuple-element.8.refs_2_, bf16[896,896]{1,0:T(8,128)(2,1)S(1)} %dense_basis.1.dense_ref.refs_3_, bf16[2048,128]{1,0:T(8,128)(2,1)S(1)} %copy-done.4, ...), custom_call_target="tpu_custom_call" | custom-call | flops 11274289152 | bytes 11010048 | tf_op jit(solution)/shard_map/half_first/pallas_call | solution.py:169
  121.3 25.5 %half_next.1 = bf16[3,2048,896]{2,1,0:T(8,128)(2,1)} custom-call(s32[8]{0:T(128)S(1)} %stack.62.refs_0_, bf16[256,2048]{1,0:T(8,128)(2,1)S(1)} %get-tuple-element.7.refs_1_, bf16[3,256,896]{2,1,0:T(8,128)(2,1)S(1)} %get-tuple-element.8.refs_2_, bf16[896,896]{1,0:T(8,128)(2,1)S(1)} %dense_basis.1.dense_ref.refs_3_, ...), custom_call_target="tpu_custom_call" | custom-call | flops 11274289152 | bytes 22020096 | tf_op jit(solution)/shard_map/half_next/pallas_call | solution.py:169
  (36 shorter events, 1.9 us)
Async XLA Ops:
  2.7 8.4 %copy-start.3 = (bf16[2048,128]{1,0:T(8,128)(2,1)S(1)}, bf16[2048,128]{1,0:T(8,128)(2,1)}, u32[]{:S(2)}) copy-start(bf16[2048,128]{1,0:T(8,128)(2,1)} %refs_4_.1) | copy-start | bytes 1572868
  2.7 73.7 %copy-start.2 = (bf16[4,224,224]{2,1,0:T(8,128)(2,1)S(1)}, bf16[4,224,224]{2,1,0:T(8,128)(2,1)}, u32[]{:S(2)}) copy-start(bf16[4,224,224]{2,1,0:T(8,128)(2,1)} %blocks_ref.1) | copy-start | bytes 1204228
  3.7 33.7 %all-to-all-start = ((bf16[8,16,3968]{2,1,0:T(8,128)(2,1)}), bf16[8,16,3968]{2,1,0:T(8,128)(2,1)S(1)}, u32[]{:S(2)}, u32[]{:S(2)}) async-start(bf16[8,16,3968]{2,1,0:T(8,128)(2,1)} %pad_maximum_fusion), calls=%async_computation | async-start | bytes 2031616 | tf_op jit(solution)/shard_map/all_to_all | solution.py:232
  11.0 47.6 %collective-permute-start.1 = (bf16[2048,128]{1,0:T(8,128)(2,1)S(1)}, bf16[2048,128]{1,0:T(8,128)(2,1)}, u32[]{:S(2)}, u32[]{:S(2)}) collective-permute-start(bf16[2048,128]{1,0:T(8,128)(2,1)S(1)} %copy-done.3), channel_id=1, source_target_pairs={{0,4},{1,5},{2,6},{3,7},{4,12},{5,13},{6,14},{7,15},{8,0},{9,1},{1... | collective-permute-start | bytes 1572872 | tf_op jit(solution)/shard_map/ppermute | solution.py:221
  13.1 47.0 %collective-permute-start.10 = (bf16[2048,128]{1,0:T(8,128)(2,1)S(1)}, bf16[2048,128]{1,0:T(8,128)(2,1)}, u32[]{:S(2)}, u32[]{:S(2)}) collective-permute-start(bf16[2048,128]{1,0:T(8,128)(2,1)S(1)} %copy-done.3), channel_id=1, source_target_pairs={{0,2},{1,3},{2,0},{3,1},{4,6},{5,7},{6,4},{7,5},{8,10},{9,11},{10,... | collective-permute-start | bytes 1572872 | tf_op jit(solution)/shard_map/ppermute | solution.py:221
  37.5 37.8 %collective-permute-start = (bf16[128,3968]{1,0:T(8,128)(2,1)S(1)}, bf16[128,3968]{1,0:T(8,128)(2,1)S(1)}, u32[]{:S(2)}, u32[]{:S(2)}) collective-permute-start(bf16[128,3968]{1,0:T(8,128)(2,1)S(1)} %bitcast.25), channel_id=1, source_target_pairs={{0,1},{1,0},{2,3},{3,2},{4,5},{5,4},{6,7},{7,6},{8,9},{9,8},{10,11... | collective-permute-start | bytes 3047432 | tf_op jit(solution)/shard_map/ppermute | solution.py:221
  37.5 22.6 %collective-permute-start.6 = (bf16[2048,128]{1,0:T(8,128)(2,1)S(1)}, bf16[2048,128]{1,0:T(8,128)(2,1)}, u32[]{:S(2)}, u32[]{:S(2)}) collective-permute-start(bf16[2048,128]{1,0:T(8,128)(2,1)S(1)} %copy-done.3), channel_id=1, source_target_pairs={{4,0},{5,1},{6,2},{7,3},{12,4},{13,5},{14,6},{15,7},{0,8},{1,9},{2... | collective-permute-start | bytes 1572872 | tf_op jit(solution)/shard_map/ppermute | solution.py:221
  37.5 22.7 %collective-permute-start.11 = (bf16[2048,128]{1,0:T(8,128)(2,1)S(1)}, bf16[2048,128]{1,0:T(8,128)(2,1)S(1)}, u32[]{:S(2)}, u32[]{:S(2)}) collective-permute-start(bf16[2048,128]{1,0:T(8,128)(2,1)S(1)} %copy-done.3), channel_id=1, source_target_pairs={{0,1},{1,0},{2,3},{3,2},{4,5},{5,4},{6,7},{7,6},{8,9},{9,8},{10,11... | collective-permute-start | bytes 1572872 | tf_op jit(solution)/shard_map/ppermute | solution.py:221
  58.7 15.1 %collective-permute-start.13 = (bf16[2048,128]{1,0:T(8,128)(2,1)}, bf16[2048,128]{1,0:T(8,128)(2,1)}, u32[]{:S(2)}, u32[]{:S(2)}) collective-permute-start(bf16[2048,128]{1,0:T(8,128)(2,1)} %collective-permute-done.1.refs_8_), channel_id=1, source_target_pairs={{0,2},{1,3},{2,0},{3,1},{4,6},{5,7},{6,4},{7,5},{8,10},{9,11},{10,... | collective-permute-start | bytes 1572872 | tf_op jit(solution)/shard_map/ppermute | solution.py:221
  60.1 13.9 %collective-permute-start.2 = (bf16[2048,128]{1,0:T(8,128)(2,1)}, bf16[2048,128]{1,0:T(8,128)(2,1)}, u32[]{:S(2)}, u32[]{:S(2)}) collective-permute-start(bf16[2048,128]{1,0:T(8,128)(2,1)} %collective-permute-done.1.refs_8_), channel_id=1, source_target_pairs={{0,4},{1,5},{2,6},{3,7},{4,12},{5,13},{6,14},{7,15},{8,0},{9,1},{1... | collective-permute-start | bytes 1572872 | tf_op jit(solution)/shard_map/ppermute | solution.py:221
  60.1 18.4 %collective-permute-start.12 = (bf16[2048,128]{1,0:T(8,128)(2,1)}, bf16[2048,128]{1,0:T(8,128)(2,1)}, u32[]{:S(2)}, u32[]{:S(2)}) collective-permute-start(bf16[2048,128]{1,0:T(8,128)(2,1)} %collective-permute-done.10.refs_5_), channel_id=1, source_target_pairs={{0,1},{1,0},{2,3},{3,2},{4,5},{5,4},{6,7},{7,6},{8,9},{9,8},{10,11... | collective-permute-start | bytes 1572872 | tf_op jit(solution)/shard_map/ppermute | solution.py:221
  60.2 0.8 copy-start.5
  61.0 24.0 %collective-permute-start.7 = (bf16[2048,128]{1,0:T(8,128)(2,1)}, bf16[2048,128]{1,0:T(8,128)(2,1)}, u32[]{:S(2)}, u32[]{:S(2)}) collective-permute-start(bf16[2048,128]{1,0:T(8,128)(2,1)} %collective-permute-done.6.refs_8_), channel_id=1, source_target_pairs={{0,2},{1,3},{2,0},{3,1},{4,6},{5,7},{6,4},{7,5},{8,10},{9,11},{10,... | collective-permute-start | bytes 1572872 | tf_op jit(solution)/shard_map/ppermute | solution.py:221
  73.8 11.2 %collective-permute-start.14 = (bf16[2048,128]{1,0:T(8,128)(2,1)}, bf16[2048,128]{1,0:T(8,128)(2,1)}, u32[]{:S(2)}, u32[]{:S(2)}) collective-permute-start(bf16[2048,128]{1,0:T(8,128)(2,1)} %collective-permute-done.1.refs_8_), channel_id=1, source_target_pairs={{0,1},{1,0},{2,3},{3,2},{4,5},{5,4},{6,7},{7,6},{8,9},{9,8},{10,11... | collective-permute-start | bytes 1572872 | tf_op jit(solution)/shard_map/ppermute | solution.py:221
  74.0 20.1 %collective-permute-start.3 = (bf16[2048,128]{1,0:T(8,128)(2,1)}, bf16[2048,128]{1,0:T(8,128)(2,1)}, u32[]{:S(2)}, u32[]{:S(2)}) collective-permute-start(bf16[2048,128]{1,0:T(8,128)(2,1)} %collective-permute-done.2.refs_4_), channel_id=1, source_target_pairs={{0,2},{1,3},{2,0},{3,1},{4,6},{5,7},{6,4},{7,5},{8,10},{9,11},{10,... | collective-permute-start | bytes 1572872 | tf_op jit(solution)/shard_map/ppermute | solution.py:221
  75.2 1.0 copy-start
  76.2 17.9 %collective-permute-start.15 = (bf16[2048,128]{1,0:T(8,128)(2,1)}, bf16[2048,128]{1,0:T(8,128)(2,1)}, u32[]{:S(2)}, u32[]{:S(2)}) collective-permute-start(bf16[2048,128]{1,0:T(8,128)(2,1)} %collective-permute-done.13.refs_9_), channel_id=1, source_target_pairs={{0,1},{1,0},{2,3},{3,2},{4,5},{5,4},{6,7},{7,6},{8,9},{9,8},{10,11... | collective-permute-start | bytes 1572872 | tf_op jit(solution)/shard_map/ppermute | solution.py:221
  76.8 1.2 copy-start.1
  78.5 42.8 %collective-permute-start.8 = (bf16[2048,128]{1,0:T(8,128)(2,1)}, bf16[2048,128]{1,0:T(8,128)(2,1)S(1)}, u32[]{:S(2)}, u32[]{:S(2)}) collective-permute-start(bf16[2048,128]{1,0:T(8,128)(2,1)} %collective-permute-done.6.refs_8_), channel_id=1, source_target_pairs={{0,1},{1,0},{2,3},{3,2},{4,5},{5,4},{6,7},{7,6},{8,9},{9,8},{10,11... | collective-permute-start | bytes 1572872 | tf_op jit(solution)/shard_map/ppermute | solution.py:221
  85.0 36.3 %collective-permute-start.4 = (bf16[2048,128]{1,0:T(8,128)(2,1)}, bf16[2048,128]{1,0:T(8,128)(2,1)S(1)}, u32[]{:S(2)}, u32[]{:S(2)}) collective-permute-start(bf16[2048,128]{1,0:T(8,128)(2,1)} %collective-permute-done.2.refs_4_), channel_id=1, source_target_pairs={{0,1},{1,0},{2,3},{3,2},{4,5},{5,4},{6,7},{7,6},{8,9},{9,8},{10,11... | collective-permute-start | bytes 1572872 | tf_op jit(solution)/shard_map/ppermute | solution.py:221
  85.0 36.3 %collective-permute-start.9 = (bf16[2048,128]{1,0:T(8,128)(2,1)}, bf16[2048,128]{1,0:T(8,128)(2,1)S(1)}, u32[]{:S(2)}, u32[]{:S(2)}) collective-permute-start(bf16[2048,128]{1,0:T(8,128)(2,1)} %collective-permute-done.7.refs_9_), channel_id=1, source_target_pairs={{0,1},{1,0},{2,3},{3,2},{4,5},{5,4},{6,7},{7,6},{8,9},{9,8},{10,11... | collective-permute-start | bytes 1572872 | tf_op jit(solution)/shard_map/ppermute | solution.py:221
  94.1 27.2 %collective-permute-start.5 = (bf16[2048,128]{1,0:T(8,128)(2,1)}, bf16[2048,128]{1,0:T(8,128)(2,1)S(1)}, u32[]{:S(2)}, u32[]{:S(2)}) collective-permute-start(bf16[2048,128]{1,0:T(8,128)(2,1)} %collective-permute-done.3.refs_5_), channel_id=1, source_target_pairs={{0,1},{1,0},{2,3},{3,2},{4,5},{5,4},{6,7},{7,6},{8,9},{9,8},{10,11... | collective-permute-start | bytes 1572872 | tf_op jit(solution)/shard_map/ppermute | solution.py:221
  94.1 1.0 copy-start.4
  95.1 1.0 copy-start.6

commit v3 on v2

--- a/solution.py
+++ b/solution.py
@@ -25,21 +25,26 @@
     return out
 
 
-def basis_kernel(blocks_ref, dense_ref):
+def basis_kernel(where_ref, blocks_ref, dense_ref):
+    del where_ref
     count, order, _ = blocks_ref.shape
     dense_ref[...] = jnp.zeros_like(dense_ref)
     for b in range(count):
         dense_ref[b * order : (b + 1) * order, b * order : (b + 1) * order] = blocks_ref[b]
 
 
-def block_diagonal(blocks):
+def block_diagonal(where, blocks):
     count, order, _ = blocks.shape
     return pl.pallas_call(
         basis_kernel,
+        in_specs=[
+            pl.BlockSpec(memory_space=pltpu.SMEM),
+            pl.BlockSpec(blocks.shape, lambda: (0, 0, 0)),
+        ],
         out_shape=jax.ShapeDtypeStruct((count * order,) * 2, blocks.dtype),
         compiler_params=pltpu.CompilerParams(vmem_limit_bytes=8 << 20),
         name="dense_basis",
-    )(blocks)
+    )(where, blocks)
 
 
 def tokens_kernel(order, core_ref, got_ref, swap_ref, dense_ref, sel_ref, og_ref):
@@ -47,7 +52,7 @@
     units = og_ref.shape[1]
     width = dense_ref.shape[0]
     shared = got_ref.shape[1] - units - LANES
-    at = pl.ds(pl.multiple_of(core_ref[0] * width, LANES), width)
+    at = pl.ds(pl.multiple_of(core_ref[2] * width, LANES), width)
     for i, ref in enumerate((got_ref, swap_ref)):
         rows = slice(i * half, (i + 1) * half)
         og_ref[rows, :] = ref[:, shared : shared + units]
@@ -66,22 +71,15 @@
 def tokens_of(order, core, got, swapped, dense, units):
     half = got.shape[0]
     width = dense.shape[0]
+    whole = pl.BlockSpec(memory_space=pltpu.VMEM)
     return pl.pallas_call(
         functools.partial(tokens_kernel, order),
         out_shape=(
             jax.ShapeDtypeStruct((QUERIES, 2 * half, width), jnp.bfloat16),
             jax.ShapeDtypeStruct((2 * half, units), jnp.bfloat16),
         ),
-        in_specs=[
-            pl.BlockSpec(memory_space=pltpu.SMEM),
-            pl.BlockSpec(got.shape, lambda: (0, 0)),
-            pl.BlockSpec(swapped.shape, lambda: (0, 0)),
-            pl.BlockSpec(dense.shape, lambda: (0, 0)),
-        ],
-        out_specs=(
-            pl.BlockSpec((QUERIES, 2 * half, width), lambda: (0, 0, 0)),
-            pl.BlockSpec((2 * half, units), lambda: (0, 0)),
-        ),
+        in_specs=[pl.BlockSpec(memory_space=pltpu.SMEM), whole, whole, whole],
+        out_specs=(whole, whole),
         compiler_params=pltpu.CompilerParams(vmem_limit_bytes=20 << 20),
         cost_estimate=pl.CostEstimate(
             flops=4 * half * width * width, bytes_accessed=4 << 20, transcendentals=0
@@ -90,8 +88,8 @@
     )(core, got, swapped, dense)
 
 
-def half_kernel(order, first, count, *refs):
-    ids_ref, og_ref, sel_ref, dense_ref = refs[:4]
+def half_kernel(order, first, count, sources, *refs):
+    where_ref, og_ref, sel_ref, dense_ref = refs[:4]
     basis_refs = refs[4 : 4 + count]
     eig_ref = refs[4 + count]
     if first:
@@ -105,13 +103,22 @@
 
     @pl.when(step == 0)
     def _():
+        z, y, c = where_ref[0], where_ref[1], where_ref[2]
+        level_z = [
+            sum(jnp.where(z == i, v, 0) for i, v in enumerate(table)) for table in sources
+        ]
+
         def fetch(j):
-            at = pl.ds(pl.multiple_of(ids_ref[j] * shard, shard), shard)
+            yy = y if j % 2 == 0 else 1 - y
+            cc = c if j % 4 < 2 else 1 - c
+            place = (level_z[j // 4] * 2 + yy) * 2 + cc
+            at = pl.ds(pl.multiple_of(place * shard, shard), shard)
             to = pl.ds(pl.multiple_of(j * shard, shard), shard)
             return pltpu.make_async_copy(eig_ref.at[at, :], inv_ref.at[to, :], sems.at[j])
 
-        for j in range(count):
-            fetch(j).start()
+        fetches = [fetch(j) for j in range(count)]
+        for f in fetches:
+            f.start()
         for j in range(0, count, 2):
             basis = jnp.concatenate([r[...] for r in basis_refs[j : j + 2]], axis=1)
             rg = jnp.dot(og_ref[...], basis, preferred_element_type=jnp.float32)
@@ -119,8 +126,11 @@
 
         @pl.loop(0, count // 2)
         def _(i):
-            fetch(2 * i).wait()
-            fetch(2 * i + 1).wait()
+            for j in (2 * i, 2 * i + 1):
+                to = pl.ds(pl.multiple_of(j * shard, shard), shard)
+                pltpu.make_async_copy(
+                    eig_ref.at[0:shard, :], inv_ref.at[to, :], sems.at[j]
+                ).wait()
             at = pl.ds(pl.multiple_of(i * 2 * shard, 2 * shard), 2 * shard)
             inv = 1.0 / inv_ref[at, :]
             for q in range(QUERIES):
@@ -145,7 +155,7 @@
         out_ref[q] = own.astype(out_ref.dtype)
 
 
-def half_of(order, shard_ids, og, sel, dense, bases, eig, acc):
+def half_of(order, sources, where, og, sel, dense, bases, eig, acc):
     tokens, units = og.shape
     width = sel.shape[2]
     shard = bases[0].shape[1]
@@ -153,12 +163,7 @@
     rows = min(units, ROWS)
     first = acc is None
     whole = pl.BlockSpec(memory_space=pltpu.VMEM)
-    once = pl.Buffered(1)
-    in_specs = [
-        pl.BlockSpec(og.shape, lambda i, s: (0, 0), pipeline_mode=once),
-        pl.BlockSpec(sel.shape, lambda i, s: (0, 0, 0), pipeline_mode=once),
-        pl.BlockSpec(dense.shape, lambda i, s: (0, 0), pipeline_mode=once),
-    ]
+    in_specs = [whole] * 3
     in_specs += [whole] * count
     in_specs.append(pl.BlockSpec(memory_space=pltpu.HBM))
     out_block = pl.BlockSpec((QUERIES, rows, width), lambda i, s: (0, i, 0))
@@ -167,7 +172,7 @@
         in_specs.append(out_block)
         args.append(pltpu.with_memory_space_constraint(acc, pltpu.HBM))
     return pl.pallas_call(
-        functools.partial(half_kernel, order, first, count),
+        functools.partial(half_kernel, order, first, count, sources),
         out_shape=pltpu.HBM((QUERIES, units, width), jnp.bfloat16),
         grid_spec=pltpu.PrefetchScalarGridSpec(
             num_scalar_prefetch=1,
@@ -190,7 +195,7 @@
             transcendentals=0,
         ),
         name="half_first" if first else "half_next",
-    )(shard_ids, *args)
+    )(where, *args)
 
 
 def ring_of(nz):
@@ -220,6 +225,8 @@
     perm_zr = [(t, s) for s, t in perm_z]
     move = lambda v, p: lax.ppermute(v, AXES, p)
 
+    where = jnp.stack([lax.axis_index(a) for a in AXES[1:]]).astype(jnp.int32)
+
     ids = jnp.broadcast_to(query_ids.astype(jnp.bfloat16)[:, None], (tokens, LANES))
     common = jnp.concatenate([out_grads, ids], axis=1)
     parcels = jnp.concatenate(
@@ -245,23 +252,19 @@
         far_across = move(across, perm_core)
         levels.append((along[k], across, far, far_across))
 
-    z, y, c = lax.axis_index("z"), lax.axis_index("y"), lax.axis_index("c")
-    dense = block_diagonal(act_basis)
-    sel, og = tokens_of(
-        order, c.astype(jnp.int32)[None], got, swapped, dense, units
-    )
-
-    ids_at, level_z = [], list(range(nz))
+    dense = block_diagonal(where, act_basis)
+    sel, og = tokens_of(order, where, got, swapped, dense, units)
+    sources, level_z = [], list(range(nz))
     for _ in range(nz):
-        zk = sum(jnp.where(z == i, v, 0) for i, v in enumerate(level_z))
-        ids_at.append([(zk * ny + yy) * nc + cc for cc in (c, 1 - c) for yy in (y, 1 - y)])
+        sources.append(tuple(level_z))
         level_z = [before[v] for v in level_z]
     acc = None
     for k in range(0, nz, nz // 2):
         span = range(k, k + nz // 2)
-        shard_ids = jnp.stack([i for j in span for i in ids_at[j]]).astype(jnp.int32)
         bases = [b for j in span for b in levels[j]]
-        acc = half_of(order, shard_ids, og, sel, dense, bases, eigenvalues, acc)
+        acc = half_of(
+            order, [sources[j] for j in span], where, og, sel, dense, bases, eigenvalues, acc
+        )
     return acc
 
 

time: 148 us -> 146 us (0.986)
  local copies, waits for them, and re-layouts: 6.4 us -> 1.97 us
  Pallas kernels: 51.3 us -> 52.9 us
    unnamed x14 -> x8, local copies, waits for them, and re-layouts: 5.06 us -> 0.81 us
  transfers between devices with their start and end apart: 17 -> 17, of which waited for: 6 -> 6; matrix products, arithmetic and copies ran while one was open for 0% -> 0% of each run, Pallas kernels for 18% -> 19%
where the time goes in v3:
time: 146 us; the launch traced here: 145 us
  waiting for transfers between devices  71.9 us (49%)
  Pallas kernels  52.9 us (36%)
  starting transfers between devices  15.7 us (11%)
  other arithmetic  2.6 us (2%)
  local copies, waits for them, and re-layouts  1.97 us (1%)
    pallas_call x2, Pallas kernels, half_of(): pl.pallas_call(functools.partial(half_kernel, order, first, count, source...  51 us
    ppermute x16, waiting for transfers between devices, streamed(): move = lambda v, p: lax.ppermute(v, AXES, p)  48.9 us
    all_to_all x1, waiting for transfers between devices, streamed(): lax.all_to_all(parcels, ('z', 'y'), split_axis=0, concat_axis=0, tiled=True)  22.9 us
    ppermute x16, starting transfers between devices, streamed(): move = lambda v, p: lax.ppermute(v, AXES, p)  8.43 us
    all_to_all x1, starting transfers between devices, streamed(): lax.all_to_all(parcels, ('z', 'y'), split_axis=0, concat_axis=0, tiled=True)  7.31 us
  transfers between devices with their start and end apart: 17, of which 6 were waited for; matrix products, arithmetic and copies ran while one was open for 0% of the time, Pallas kernels for 19%

profile of v3, /device:TPU:0, one launch (start us, length us, event | category | flops | bytes accessed | tf_op | source)
XLA Modules:
  0.0 145.2 jit_solution(12863332305566353320)
XLA Ops:
  0.0 0.7 convert_element_type.3
  0.7 1.0 copy.10
  1.8 0.8 pad_maximum_fusion.1
  2.7 1.0 pad_maximum_fusion
  3.7 7.3 %all-to-all-start = ((bf16[8,16,3968]{2,1,0:T(8,128)(2,1)}), bf16[8,16,3968]{2,1,0:T(8,128)(2,1)S(1)}, u32[]{:S(2)}, u32[]{:S(2)}) async-start(bf16[8,16,3968]{2,1,0:T(8,128)(2,1)} %pad_maximum_fusion), calls=%async_computation | async-start | bytes 2031616 | tf_op jit(solution)/shard_map/all_to_all | solution.py:239
  11.0 2.0 %collective-permute-start.1 = (bf16[2048,128]{1,0:T(8,128)(2,1)S(1)}, bf16[2048,128]{1,0:T(8,128)(2,1)}, u32[]{:S(2)}, u32[]{:S(2)}) collective-permute-start(bf16[2048,128]{1,0:T(8,128)(2,1)S(1)} %copy-done.1), channel_id=1, source_target_pairs={{0,4},{1,5},{2,6},{3,7},{4,12},{5,13},{6,14},{7,15},{8,0},{9,1},{1... | collective-permute-start | bytes 1572872 | tf_op jit(solution)/shard_map/ppermute | solution.py:226
  13.1 1.5 %collective-permute-start.10 = (bf16[2048,128]{1,0:T(8,128)(2,1)S(1)}, bf16[2048,128]{1,0:T(8,128)(2,1)}, u32[]{:S(2)}, u32[]{:S(2)}) collective-permute-start(bf16[2048,128]{1,0:T(8,128)(2,1)S(1)} %copy-done.1), channel_id=1, source_target_pairs={{0,2},{1,3},{2,0},{3,1},{4,6},{5,7},{6,4},{7,5},{8,10},{9,11},{10,... | collective-permute-start | bytes 1572872 | tf_op jit(solution)/shard_map/ppermute | solution.py:226
  14.5 22.9 %all-to-all-done = bf16[8,16,3968]{2,1,0:T(8,128)(2,1)S(1)} async-done(((bf16[8,16,3968]{2,1,0:T(8,128)(2,1)}), bf16[8,16,3968]{2,1,0:T(8,128)(2,1)S(1)}, u32[]{:S(2)}, u32[]{:S(2)}) %all-to-all-start) | async-done | bytes 1015840 | tf_op jit(solution)/shard_map/all_to_all | solution.py:239
  37.5 0.5 collective-permute-start.11
  38.0 20.7 %collective-permute-done.1.refs_8_ = bf16[2048,128]{1,0:T(8,128)(2,1)} collective-permute-done((bf16[2048,128]{1,0:T(8,128)(2,1)S(1)}, bf16[2048,128]{1,0:T(8,128)(2,1)}, u32[]{:S(2)}, u32[]{:S(2)}) %collective-permute-start.1) | collective-permute-done | bytes 524320 | tf_op jit(solution)/shard_map/ppermute | solution.py:226
  58.7 1.4 collective-permute-start.13
  60.2 0.8 copy-done.2
  61.0 0.6 collective-permute-start.7
  61.6 12.2 %collective-permute-done.13.refs_9_ = bf16[2048,128]{1,0:T(8,128)(2,1)} collective-permute-done((bf16[2048,128]{1,0:T(8,128)(2,1)}, bf16[2048,128]{1,0:T(8,128)(2,1)}, u32[]{:S(2)}, u32[]{:S(2)}) %collective-permute-start.13) | collective-permute-done | bytes 524320 | tf_op jit(solution)/shard_map/ppermute | solution.py:226
  74.0 1.2 collective-permute-start.3
  75.2 0.2 collective-permute-start.15
  75.5 0.7 dense_basis.1.dense_ref.refs_3_
  76.3 1.1 tokens.1
  77.4 0.4 collective-permute-start.8
  77.7 7.3 %collective-permute-done.7.refs_9_ = bf16[2048,128]{1,0:T(8,128)(2,1)} collective-permute-done((bf16[2048,128]{1,0:T(8,128)(2,1)S(1)}, bf16[2048,128]{1,0:T(8,128)(2,1)}, u32[]{:S(2)}, u32[]{:S(2)}) %collective-permute-start.7) | collective-permute-done | bytes 524320 | tf_op jit(solution)/shard_map/ppermute | solution.py:226
  85.0 0.5 collective-permute-start.9
  85.5 8.5 %collective-permute-done.3.refs_5_ = bf16[2048,128]{1,0:T(8,128)(2,1)} collective-permute-done((bf16[2048,128]{1,0:T(8,128)(2,1)}, bf16[2048,128]{1,0:T(8,128)(2,1)}, u32[]{:S(2)}, u32[]{:S(2)}) %collective-permute-start.3) | collective-permute-done | bytes 524320 | tf_op jit(solution)/shard_map/ppermute | solution.py:226
  94.1 25.3 %half_first.1.refs_13_ = bf16[3,2048,896]{2,1,0:T(8,128)(2,1)} custom-call(s32[3]{0:T(128)S(1)} %pad_add_fusion.where_ref.core_ref.refs_0_, bf16[256,2048]{1,0:T(8,128)(2,1)S(1)} %get-tuple-element.7.refs_1_, bf16[3,256,896]{2,1,0:T(8,128)(2,1)S(1)} %get-tuple-element.8.refs_2_, bf16[896,896]{1,0:T(8,128)(2,1)S(1)} %dense_basis.1.dense_ref.refs_3_, ...), custom_call_target="tpu_custom_call" | custom-call | flops 11274289152 | bytes 11010048 | tf_op jit(solution)/shard_map/half_first/pallas_call | solution.py:174
  119.5 25.7 %half_next.1 = bf16[3,2048,896]{2,1,0:T(8,128)(2,1)} custom-call(s32[3]{0:T(128)S(1)} %pad_add_fusion.where_ref.core_ref.refs_0_, bf16[256,2048]{1,0:T(8,128)(2,1)S(1)} %get-tuple-element.7.refs_1_, bf16[3,256,896]{2,1,0:T(8,128)(2,1)S(1)} %get-tuple-element.8.refs_2_, bf16[896,896]{1,0:T(8,128)(2,1)S(1)} %dense_basis.1.dense_ref.refs_3_, ...), custom_call_target="tpu_custom_call" | custom-call | flops 11274289152 | bytes 22020096 | tf_op jit(solution)/shard_map/half_next/pallas_call | solution.py:174
  (29 shorter events, 0.5 us)
Async XLA Ops:
  2.7 8.4 %copy-start.1 = (bf16[2048,128]{1,0:T(8,128)(2,1)S(1)}, bf16[2048,128]{1,0:T(8,128)(2,1)}, u32[]{:S(2)}) copy-start(bf16[2048,128]{1,0:T(8,128)(2,1)} %refs_4_.1) | copy-start | bytes 1572868
  2.7 72.8 %copy-start = (bf16[4,224,224]{2,1,0:T(8,128)(2,1)S(1)}, bf16[4,224,224]{2,1,0:T(8,128)(2,1)}, u32[]{:S(2)}) copy-start(bf16[4,224,224]{2,1,0:T(8,128)(2,1)} %blocks_ref.1) | copy-start | bytes 1204228
  3.7 33.7 %all-to-all-start = ((bf16[8,16,3968]{2,1,0:T(8,128)(2,1)}), bf16[8,16,3968]{2,1,0:T(8,128)(2,1)S(1)}, u32[]{:S(2)}, u32[]{:S(2)}) async-start(bf16[8,16,3968]{2,1,0:T(8,128)(2,1)} %pad_maximum_fusion), calls=%async_computation | async-start | bytes 2031616 | tf_op jit(solution)/shard_map/all_to_all | solution.py:239
  11.0 47.6 %collective-permute-start.1 = (bf16[2048,128]{1,0:T(8,128)(2,1)S(1)}, bf16[2048,128]{1,0:T(8,128)(2,1)}, u32[]{:S(2)}, u32[]{:S(2)}) collective-permute-start(bf16[2048,128]{1,0:T(8,128)(2,1)S(1)} %copy-done.1), channel_id=1, source_target_pairs={{0,4},{1,5},{2,6},{3,7},{4,12},{5,13},{6,14},{7,15},{8,0},{9,1},{1... | collective-permute-start | bytes 1572872 | tf_op jit(solution)/shard_map/ppermute | solution.py:226
  13.1 47.0 %collective-permute-start.10 = (bf16[2048,128]{1,0:T(8,128)(2,1)S(1)}, bf16[2048,128]{1,0:T(8,128)(2,1)}, u32[]{:S(2)}, u32[]{:S(2)}) collective-permute-start(bf16[2048,128]{1,0:T(8,128)(2,1)S(1)} %copy-done.1), channel_id=1, source_target_pairs={{0,2},{1,3},{2,0},{3,1},{4,6},{5,7},{6,4},{7,5},{8,10},{9,11},{10,... | collective-permute-start | bytes 1572872 | tf_op jit(solution)/shard_map/ppermute | solution.py:226
  37.5 37.8 %collective-permute-start = (bf16[128,3968]{1,0:T(8,128)(2,1)S(1)}, bf16[128,3968]{1,0:T(8,128)(2,1)S(1)}, u32[]{:S(2)}, u32[]{:S(2)}) collective-permute-start(bf16[128,3968]{1,0:T(8,128)(2,1)S(1)} %bitcast.11), channel_id=1, source_target_pairs={{0,1},{1,0},{2,3},{3,2},{4,5},{5,4},{6,7},{7,6},{8,9},{9,8},{10,11... | collective-permute-start | bytes 3047432 | tf_op jit(solution)/shard_map/ppermute | solution.py:226
  37.5 22.6 %collective-permute-start.6 = (bf16[2048,128]{1,0:T(8,128)(2,1)S(1)}, bf16[2048,128]{1,0:T(8,128)(2,1)S(1)}, u32[]{:S(2)}, u32[]{:S(2)}) collective-permute-start(bf16[2048,128]{1,0:T(8,128)(2,1)S(1)} %copy-done.1), channel_id=1, source_target_pairs={{4,0},{5,1},{6,2},{7,3},{12,4},{13,5},{14,6},{15,7},{0,8},{1,9},{2... | collective-permute-start | bytes 1572872 | tf_op jit(solution)/shard_map/ppermute | solution.py:226
  37.5 22.7 %collective-permute-start.11 = (bf16[2048,128]{1,0:T(8,128)(2,1)S(1)}, bf16[2048,128]{1,0:T(8,128)(2,1)S(1)}, u32[]{:S(2)}, u32[]{:S(2)}) collective-permute-start(bf16[2048,128]{1,0:T(8,128)(2,1)S(1)} %copy-done.1), channel_id=1, source_target_pairs={{0,1},{1,0},{2,3},{3,2},{4,5},{5,4},{6,7},{7,6},{8,9},{9,8},{10,11... | collective-permute-start | bytes 1572872 | tf_op jit(solution)/shard_map/ppermute | solution.py:226
  58.7 15.1 %collective-permute-start.13 = (bf16[2048,128]{1,0:T(8,128)(2,1)}, bf16[2048,128]{1,0:T(8,128)(2,1)}, u32[]{:S(2)}, u32[]{:S(2)}) collective-permute-start(bf16[2048,128]{1,0:T(8,128)(2,1)} %collective-permute-done.1.refs_8_), channel_id=1, source_target_pairs={{0,2},{1,3},{2,0},{3,1},{4,6},{5,7},{6,4},{7,5},{8,10},{9,11},{10,... | collective-permute-start | bytes 1572872 | tf_op jit(solution)/shard_map/ppermute | solution.py:226
  60.1 13.9 %collective-permute-start.2 = (bf16[2048,128]{1,0:T(8,128)(2,1)}, bf16[2048,128]{1,0:T(8,128)(2,1)}, u32[]{:S(2)}, u32[]{:S(2)}) collective-permute-start(bf16[2048,128]{1,0:T(8,128)(2,1)} %collective-permute-done.1.refs_8_), channel_id=1, source_target_pairs={{0,4},{1,5},{2,6},{3,7},{4,12},{5,13},{6,14},{7,15},{8,0},{9,1},{1... | collective-permute-start | bytes 1572872 | tf_op jit(solution)/shard_map/ppermute | solution.py:226
  60.1 17.3 %collective-permute-start.12 = (bf16[2048,128]{1,0:T(8,128)(2,1)}, bf16[2048,128]{1,0:T(8,128)(2,1)}, u32[]{:S(2)}, u32[]{:S(2)}) collective-permute-start(bf16[2048,128]{1,0:T(8,128)(2,1)} %collective-permute-done.10.refs_5_), channel_id=1, source_target_pairs={{0,1},{1,0},{2,3},{3,2},{4,5},{5,4},{6,7},{7,6},{8,9},{9,8},{10,11... | collective-permute-start | bytes 1572872 | tf_op jit(solution)/shard_map/ppermute | solution.py:226
  60.2 0.8 copy-start.2
  61.0 24.0 %collective-permute-start.7 = (bf16[2048,128]{1,0:T(8,128)(2,1)S(1)}, bf16[2048,128]{1,0:T(8,128)(2,1)}, u32[]{:S(2)}, u32[]{:S(2)}) collective-permute-start(bf16[2048,128]{1,0:T(8,128)(2,1)S(1)} %collective-permute-done.6.refs_8_), channel_id=1, source_target_pairs={{0,2},{1,3},{2,0},{3,1},{4,6},{5,7},{6,4},{7,5},{8,10},{9,11},{10,... | collective-permute-start | bytes 1572872 | tf_op jit(solution)/shard_map/ppermute | solution.py:226
  73.8 11.2 %collective-permute-start.14 = (bf16[2048,128]{1,0:T(8,128)(2,1)}, bf16[2048,128]{1,0:T(8,128)(2,1)}, u32[]{:S(2)}, u32[]{:S(2)}) collective-permute-start(bf16[2048,128]{1,0:T(8,128)(2,1)} %collective-permute-done.1.refs_8_), channel_id=1, source_target_pairs={{0,1},{1,0},{2,3},{3,2},{4,5},{5,4},{6,7},{7,6},{8,9},{9,8},{10,11... | collective-permute-start | bytes 1572872 | tf_op jit(solution)/shard_map/ppermute | solution.py:226
  74.0 20.1 %collective-permute-start.3 = (bf16[2048,128]{1,0:T(8,128)(2,1)}, bf16[2048,128]{1,0:T(8,128)(2,1)}, u32[]{:S(2)}, u32[]{:S(2)}) collective-permute-start(bf16[2048,128]{1,0:T(8,128)(2,1)} %collective-permute-done.2.refs_4_), channel_id=1, source_target_pairs={{0,2},{1,3},{2,0},{3,1},{4,6},{5,7},{6,4},{7,5},{8,10},{9,11},{10,... | collective-permute-start | bytes 1572872 | tf_op jit(solution)/shard_map/ppermute | solution.py:226
  75.2 18.9 %collective-permute-start.15 = (bf16[2048,128]{1,0:T(8,128)(2,1)}, bf16[2048,128]{1,0:T(8,128)(2,1)}, u32[]{:S(2)}, u32[]{:S(2)}) collective-permute-start(bf16[2048,128]{1,0:T(8,128)(2,1)} %collective-permute-done.13.refs_9_), channel_id=1, source_target_pairs={{0,1},{1,0},{2,3},{3,2},{4,5},{5,4},{6,7},{7,6},{8,9},{9,8},{10,11... | collective-permute-start | bytes 1572872 | tf_op jit(solution)/shard_map/ppermute | solution.py:226
  76.3 17.8 %copy-start.3 = (bf16[2048,128]{1,0:T(8,128)(2,1)S(1)}, bf16[2048,128]{1,0:T(8,128)(2,1)}, u32[]{:S(2)}) copy-start(bf16[2048,128]{1,0:T(8,128)(2,1)} %copy-done.2) | copy-start | bytes 1572868
  77.4 42.1 %collective-permute-start.8 = (bf16[2048,128]{1,0:T(8,128)(2,1)S(1)}, bf16[2048,128]{1,0:T(8,128)(2,1)S(1)}, u32[]{:S(2)}, u32[]{:S(2)}) collective-permute-start(bf16[2048,128]{1,0:T(8,128)(2,1)S(1)} %collective-permute-done.6.refs_8_), channel_id=1, source_target_pairs={{0,1},{1,0},{2,3},{3,2},{4,5},{5,4},{6,7},{7,6},{8,9},{9,8},{10,11... | collective-permute-start | bytes 1572872 | tf_op jit(solution)/shard_map/ppermute | solution.py:226
  85.0 34.4 %collective-permute-start.4 = (bf16[2048,128]{1,0:T(8,128)(2,1)}, bf16[2048,128]{1,0:T(8,128)(2,1)S(1)}, u32[]{:S(2)}, u32[]{:S(2)}) collective-permute-start(bf16[2048,128]{1,0:T(8,128)(2,1)} %collective-permute-done.2.refs_4_), channel_id=1, source_target_pairs={{0,1},{1,0},{2,3},{3,2},{4,5},{5,4},{6,7},{7,6},{8,9},{9,8},{10,11... | collective-permute-start | bytes 1572872 | tf_op jit(solution)/shard_map/ppermute | solution.py:226
  85.0 34.4 %collective-permute-start.9 = (bf16[2048,128]{1,0:T(8,128)(2,1)}, bf16[2048,128]{1,0:T(8,128)(2,1)S(1)}, u32[]{:S(2)}, u32[]{:S(2)}) collective-permute-start(bf16[2048,128]{1,0:T(8,128)(2,1)} %collective-permute-done.7.refs_9_), channel_id=1, source_target_pairs={{0,1},{1,0},{2,3},{3,2},{4,5},{5,4},{6,7},{7,6},{8,9},{9,8},{10,11... | collective-permute-start | bytes 1572872 | tf_op jit(solution)/shard_map/ppermute | solution.py:226
  94.1 25.4 %collective-permute-start.5 = (bf16[2048,128]{1,0:T(8,128)(2,1)}, bf16[2048,128]{1,0:T(8,128)(2,1)S(1)}, u32[]{:S(2)}, u32[]{:S(2)}) collective-permute-start(bf16[2048,128]{1,0:T(8,128)(2,1)} %collective-permute-done.3.refs_5_), channel_id=1, source_target_pairs={{0,1},{1,0},{2,3},{3,2},{4,5},{5,4},{6,7},{7,6},{8,9},{9,8},{10,11... | collective-permute-start | bytes 1572872 | tf_op jit(solution)/shard_map/ppermute | solution.py:226

commit v4 on v3

--- a/solution.py
+++ b/solution.py
@@ -44,7 +44,7 @@
         out_shape=jax.ShapeDtypeStruct((count * order,) * 2, blocks.dtype),
         compiler_params=pltpu.CompilerParams(vmem_limit_bytes=8 << 20),
         name="dense_basis",
-    )(where, blocks)
+    )(where, pltpu.with_memory_space_constraint(blocks, pltpu.HBM))
 
 
 def tokens_kernel(order, core_ref, got_ref, swap_ref, dense_ref, sel_ref, og_ref):
@@ -86,6 +86,126 @@
         ),
         name="tokens",
     )(core, got, swapped, dense)
+
+
+def back_kernel(order, source, slot, *refs):
+    where_ref, og_ref, sel_ref, dense_ref = refs[:4]
+    basis_refs = refs[4:8]
+    eig_ref = refs[8]
+    rb_ref, rgt_ref, inv_ref, sems = refs[-4:]
+    count = len(basis_refs)
+    width = dense_ref.shape[0]
+    shard = basis_refs[0].shape[1]
+    z, y, c = where_ref[0], where_ref[1], where_ref[2]
+    level_z = sum(jnp.where(z == i, v, 0) for i, v in enumerate(source))
+
+    def fetch(j):
+        yy = y if j % 2 == 0 else 1 - y
+        cc = c if j % 4 < 2 else 1 - c
+        place = (level_z * 2 + yy) * 2 + cc
+        at = pl.ds(pl.multiple_of(place * shard, shard), shard)
+        to = slice(j * shard, (j + 1) * shard)
+        return pltpu.make_async_copy(eig_ref.at[at, :], inv_ref.at[to, :], sems.at[j])
+
+    fetches = [fetch(j) for j in range(count)]
+    for f in fetches:
+        f.start()
+    for j in range(0, count, 2):
+        basis = jnp.concatenate([r[...] for r in basis_refs[j : j + 2]], axis=1)
+        rg = jnp.dot(og_ref[...], basis, preferred_element_type=jnp.float32)
+        rgt_ref[j * shard : (j + 2) * shard, :] = rg.astype(jnp.bfloat16).T
+    for f in fetches:
+        f.wait()
+
+    @pl.loop(0, count // 2)
+    def _(i):
+        at = pl.ds(pl.multiple_of(i * 2 * shard, 2 * shard), 2 * shard)
+        to = pl.ds(pl.multiple_of((slot * count + 2 * i) * shard, 2 * shard), 2 * shard)
+        inv = 1.0 / inv_ref[at, :]
+        for q in range(QUERIES):
+            m = jnp.dot(rgt_ref[at, :], sel_ref[q], preferred_element_type=jnp.float32)
+            s = (m * inv).astype(jnp.bfloat16)
+            for n0, n1, k0, k1 in windows(width, order):
+                back = lax.dot_general(
+                    s[:, k0:k1],
+                    dense_ref[n0:n1, k0:k1],
+                    (((1,), (1,)), ((), ())),
+                    preferred_element_type=jnp.float32,
+                )
+                rb_ref[to, q * width + n0 : q * width + n1] = back.astype(jnp.bfloat16)
+
+
+def back_of(order, source, slot, slots, where, og, sel, dense, bases, eig, rb):
+    tokens = og.shape[0]
+    width = dense.shape[0]
+    shard = bases[0].shape[1]
+    count = len(bases)
+    whole = pl.BlockSpec(memory_space=pltpu.VMEM)
+    args = [og, sel, dense, *bases, pltpu.with_memory_space_constraint(eig, pltpu.HBM)]
+    in_specs = [pl.BlockSpec(memory_space=pltpu.SMEM)] + [whole] * (3 + count)
+    in_specs.append(pl.BlockSpec(memory_space=pltpu.HBM))
+    if rb is not None:
+        args.append(rb)
+        in_specs.append(whole)
+    return pl.pallas_call(
+        functools.partial(back_kernel, order, source, slot),
+        out_shape=jax.ShapeDtypeStruct((slots * count * shard, QUERIES * width), jnp.bfloat16),
+        in_specs=in_specs,
+        out_specs=whole,
+        scratch_shapes=[
+            pltpu.VMEM((count * shard, tokens), jnp.bfloat16),
+            pltpu.VMEM((count * shard, width), jnp.float32),
+            pltpu.SemaphoreType.DMA((count,)),
+        ],
+        input_output_aliases={} if rb is None else {len(args): 0},
+        compiler_params=pltpu.CompilerParams(vmem_limit_bytes=10 << 20),
+        cost_estimate=pl.CostEstimate(flops=5 << 30, bytes_accessed=4 << 20, transcendentals=0),
+    )(where, *args)
+
+
+def product_kernel(first, count, *refs):
+    rb_ref = refs[0]
+    basis_refs = refs[1 : 1 + count]
+    acc_ref, out_ref = (None if first else refs[1 + count]), refs[-1]
+    rows, width = out_ref.shape[1:]
+    at = pl.ds(pl.multiple_of(pl.program_id(0) * rows, rows), rows)
+    lhs = jnp.concatenate([r[at, :] for r in basis_refs], axis=1)
+    part = jnp.dot(lhs, rb_ref[...], preferred_element_type=jnp.float32)
+    for q in range(QUERIES):
+        own = part[:, q * width : (q + 1) * width]
+        if not first:
+            own = own + acc_ref[q].astype(jnp.float32)
+        out_ref[q] = own.astype(out_ref.dtype)
+
+
+def product_of(rb, bases, acc):
+    units, shard = bases[0].shape
+    count = len(bases)
+    width = rb.shape[1] // QUERIES
+    rows = min(units, 2 * ROWS)
+    first = acc is None
+    whole = pl.BlockSpec(memory_space=pltpu.VMEM)
+    out_block = pl.BlockSpec((QUERIES, rows, width), lambda i: (0, i, 0))
+    in_specs = [whole] * (1 + count)
+    args = [rb, *bases]
+    if not first:
+        in_specs.append(out_block)
+        args.append(pltpu.with_memory_space_constraint(acc, pltpu.HBM))
+    return pl.pallas_call(
+        functools.partial(product_kernel, first, count),
+        out_shape=pltpu.HBM((QUERIES, units, width), jnp.bfloat16),
+        grid=(units // rows,),
+        in_specs=in_specs,
+        out_specs=out_block,
+        compiler_params=pltpu.CompilerParams(
+            dimension_semantics=("arbitrary",), vmem_limit_bytes=24 << 20
+        ),
+        cost_estimate=pl.CostEstimate(
+            flops=2 * QUERIES * width * count * shard * units,
+            bytes_accessed=QUERIES * units * width * (2 if first else 4),
+            transcendentals=0,
+        ),
+    )(*args)
 
 
 def half_kernel(order, first, count, sources, *refs):
@@ -198,6 +318,38 @@
     )(where, *args)
 
 
+def parcel_kernel(ids_ref, act_ref, grads_ref, out_ref):
+    chips, tokens, _ = out_ref.shape
+    units = grads_ref.shape[1]
+    wide = act_ref.shape[1] // chips
+    row = lax.broadcasted_iota(jnp.int32, (tokens, LANES), 0)
+    ids = jnp.zeros((tokens, LANES), jnp.float32)
+    for t in range(tokens):
+        ids = jnp.where(row == t, ids_ref[t].astype(jnp.float32), ids)
+    ids = ids.astype(jnp.bfloat16)
+    for j in range(chips):
+        out_ref[j, :, :wide] = act_ref[:, j * wide : (j + 1) * wide]
+        out_ref[j, :, wide : wide + units] = grads_ref[...]
+        out_ref[j, :, wide + units :] = ids
+
+
+def parcels_of(chips, activations, out_grads, query_ids):
+    tokens, units = out_grads.shape
+    wide = activations.shape[1] // chips
+    return pl.pallas_call(
+        parcel_kernel,
+        out_shape=jax.ShapeDtypeStruct((chips, tokens, wide + units + LANES), jnp.bfloat16),
+        in_specs=[
+            pl.BlockSpec(memory_space=pltpu.SMEM),
+            pl.BlockSpec(activations.shape, lambda: (0, 0)),
+            pl.BlockSpec(out_grads.shape, lambda: (0, 0)),
+        ],
+        out_specs=pl.BlockSpec((chips, tokens, wide + units + LANES), lambda: (0, 0, 0)),
+        compiler_params=pltpu.CompilerParams(vmem_limit_bytes=8 << 20),
+        name="parcels",
+    )(query_ids, *(pltpu.with_memory_space_constraint(v, pltpu.HBM) for v in (activations, out_grads)))
+
+
 def ring_of(nz):
     return [0] + list(range(1, nz, 2)) + [z for z in range(nz - 1, 0, -1) if z % 2 == 0]
 
@@ -227,15 +379,7 @@
 
     where = jnp.stack([lax.axis_index(a) for a in AXES[1:]]).astype(jnp.int32)
 
-    ids = jnp.broadcast_to(query_ids.astype(jnp.bfloat16)[:, None], (tokens, LANES))
-    common = jnp.concatenate([out_grads, ids], axis=1)
-    parcels = jnp.concatenate(
-        [
-            activations.reshape(tokens, chips, nc * width).transpose(1, 0, 2),
-            jnp.broadcast_to(common[None], (chips,) + common.shape),
-        ],
-        axis=2,
-    )
+    parcels = parcels_of(chips, activations, out_grads, query_ids)
     got = lax.all_to_all(parcels, ("z", "y"), split_axis=0, concat_axis=0, tiled=True)
     got = got.reshape(chips * tokens, nc * width + units + LANES)
     swapped = move(got, perm_core)
@@ -258,14 +402,16 @@
     for _ in range(nz):
         sources.append(tuple(level_z))
         level_z = [before[v] for v in level_z]
-    acc = None
-    for k in range(0, nz, nz // 2):
-        span = range(k, k + nz // 2)
-        bases = [b for j in span for b in levels[j]]
-        acc = half_of(
-            order, [sources[j] for j in span], where, og, sel, dense, bases, eigenvalues, acc
-        )
-    return acc
+    slots = nz // 2
+    rb = None
+    for k in range(slots):
+        rb = back_of(order, sources[k], k, slots, where, og, sel, dense, levels[k], eigenvalues, rb)
+    acc = product_of(rb, [b for k in range(slots) for b in levels[k]], None)
+    rest = range(slots, nz)
+    bases = [b for k in rest for b in levels[k]]
+    return half_of(
+        order, [sources[k] for k in rest], where, og, sel, dense, bases, eigenvalues, acc
+    )
 
 
 def plain(activations, out_grads, query_ids, act_basis, grad_basis, eigenvalues):

time: 146 us -> 141 us (0.966)
  waiting for transfers between devices: 71.9 us -> 67.2 us
  Pallas kernels: 52.9 us -> 57.4 us
  other arithmetic: 2.6 us -> 0.08 us
    pallas_call x0 -> x4, Pallas kernels: none -> 29.5 us  [the longest x1 15.8 us: product_of(): pl.pallas_call(functools.partial(product_kernel, first, count), out_shape...]
    pallas_call x2 -> x1, Pallas kernels: 51 us -> 25.5 us  [half_of(): pl.pallas_call(functools.partial(half_kernel, order, first, count, source...]
    ppermute x16, waiting for transfers between devices: 48.9 us -> 42.8 us  [streamed(): move = lambda v, p: lax.ppermute(v, AXES, p)]
    concatenate x2 -> x0, other arithmetic: 1.87 us -> none  [the longest x1 1.02 us: streamed(): jnp.concatenate([activations.reshape(tokens, chips, nc * width).transpose...]
    all_to_all x1, waiting for transfers between devices: 22.9 us -> 24.4 us  [streamed(): lax.all_to_all(parcels, ('z', 'y'), split_axis=0, concat_axis=0, tiled=True)]
  transfers between devices with their start and end apart: 17 -> 17, of which waited for: 6 -> 6; matrix products, arithmetic and copies ran while one was open for 0% -> 0% of each run, Pallas kernels for 19% -> 21%
where the time goes in v4:
time: 141 us
  waiting for transfers between devices  67.2 us (48%)
  Pallas kernels  57.4 us (41%)
  starting transfers between devices  15.2 us (11%)
    ppermute x16, waiting for transfers between devices, streamed(): move = lambda v, p: lax.ppermute(v, AXES, p)  42.8 us
    pallas_call x1, Pallas kernels, half_of(): pl.pallas_call(functools.partial(half_kernel, order, first, count, source...  25.5 us
    all_to_all x1, waiting for transfers between devices, streamed(): lax.all_to_all(parcels, ('z', 'y'), split_axis=0, concat_axis=0, tiled=True)  24.4 us
    pallas_call x1, Pallas kernels, product_of(): pl.pallas_call(functools.partial(product_kernel, first, count), out_shape...  15.8 us
    pallas_call x2, Pallas kernels, back_of(): pl.pallas_call(functools.partial(back_kernel, order, source, slot), out_s...  11.7 us
    ppermute x16, starting transfers between devices, streamed(): move = lambda v, p: lax.ppermute(v, AXES, p)  7.91 us
    all_to_all x1, starting transfers between devices, streamed(): lax.all_to_all(parcels, ('z', 'y'), split_axis=0, concat_axis=0, tiled=True)  7.31 us
  transfers between devices with their start and end apart: 17, of which 6 were waited for; matrix products, arithmetic and copies ran while one was open for 0% of the time, Pallas kernels for 21%

profile of v4, /device:TPU:0, one launch (start us, length us, event | category | flops | bytes accessed | tf_op | source)
XLA Modules:
  0.0 140.6 jit_solution(10636923243212864251)
XLA Ops:
  0.0 0.7 copy-done
  0.7 2.1 %parcels.1 = bf16[8,16,3968]{2,1,0:T(8,128)(2,1)} custom-call(s32[16]{0:T(128)S(1)} %copy-done, bf16[16,14336]{1,0:T(8,128)(2,1)} %act_ref.1, bf16[16,2048]{1,0:T(8,128)(2,1)} %grads_ref.1), custom_call_target="tpu_custom_call" | custom-call | tf_op jit(solution)/shard_map/parcels/pallas_call | solution.py:339
  2.7 7.3 %all-to-all-start = ((bf16[8,16,3968]{2,1,0:T(8,128)(2,1)}), bf16[8,16,3968]{2,1,0:T(8,128)(2,1)S(1)}, u32[]{:S(2)}, u32[]{:S(2)}) async-start(bf16[8,16,3968]{2,1,0:T(8,128)(2,1)} %parcels.1), calls=%async_computation | async-start | bytes 2031616 | tf_op jit(solution)/shard_map/all_to_all | solution.py:383
  10.0 2.0 %collective-permute-start.1 = (bf16[2048,128]{1,0:T(8,128)(2,1)}, bf16[2048,128]{1,0:T(8,128)(2,1)S(1)}, u32[]{:S(2)}, u32[]{:S(2)}) collective-permute-start(bf16[2048,128]{1,0:T(8,128)(2,1)} %refs_1_.1), channel_id=1, source_target_pairs={{0,4},{1,5},{2,6},{3,7},{4,12},{5,13},{6,14},{7,15},{8,0},{9,1},{1... | collective-permute-start | bytes 1572872 | tf_op jit(solution)/shard_map/ppermute | solution.py:378
  12.0 24.4 %all-to-all-done = bf16[8,16,3968]{2,1,0:T(8,128)(2,1)S(1)} async-done(((bf16[8,16,3968]{2,1,0:T(8,128)(2,1)}), bf16[8,16,3968]{2,1,0:T(8,128)(2,1)S(1)}, u32[]{:S(2)}, u32[]{:S(2)}) %all-to-all-start) | async-done | bytes 1015840 | tf_op jit(solution)/shard_map/all_to_all | solution.py:383
  36.5 1.1 collective-permute-start.13
  37.5 20.1 %collective-permute-done.1.refs_4_.refs_5_ = bf16[2048,128]{1,0:T(8,128)(2,1)S(1)} collective-permute-done((bf16[2048,128]{1,0:T(8,128)(2,1)}, bf16[2048,128]{1,0:T(8,128)(2,1)S(1)}, u32[]{:S(2)}, u32[]{:S(2)}) %collective-permute-start.1) | collective-permute-done | bytes 524320 | tf_op jit(solution)/shard_map/ppermute | solution.py:378
  57.6 1.4 collective-permute-start.10
  59.1 0.1 pad_add_fusion.where_ref.core_ref.refs_0_
  59.2 1.3 dense_basis.1.dense_ref.refs_3_
  60.5 0.5 collective-permute-start.11
  61.0 9.2 %collective-permute-done.10.refs_5_.refs_6_ = bf16[2048,128]{1,0:T(8,128)(2,1)S(1)} collective-permute-done((bf16[2048,128]{1,0:T(8,128)(2,1)S(1)}, bf16[2048,128]{1,0:T(8,128)(2,1)S(1)}, u32[]{:S(2)}, u32[]{:S(2)}) %collective-permute-start.10) | collective-permute-done | bytes 524320 | tf_op jit(solution)/shard_map/ppermute | solution.py:378
  70.2 1.7 %collective-permute-start.7 = (bf16[2048,128]{1,0:T(8,128)(2,1)}, bf16[2048,128]{1,0:T(8,128)(2,1)S(1)}, u32[]{:S(2)}, u32[]{:S(2)}) collective-permute-start(bf16[2048,128]{1,0:T(8,128)(2,1)} %collective-permute-done.6.refs_8_), channel_id=1, source_target_pairs={{0,2},{1,3},{2,0},{3,1},{4,6},{5,7},{6,4},{7,5},{8,10},{9,11},{10,... | collective-permute-start | bytes 1572872 | tf_op jit(solution)/shard_map/ppermute | solution.py:378
  71.9 0.7 collective-permute-done.2.refs_4_
  72.6 0.3 collective-permute-start.3
  72.9 1.1 tokens.1
  74.0 0.3 collective-permute-start.8
  74.3 6.2 %shard_map.64.refs_9_ = bf16[1024,2688]{1,0:T(8,128)(2,1)S(1)} custom-call(s32[3]{0:T(128)S(1)} %pad_add_fusion.where_ref.core_ref.refs_0_, bf16[256,2048]{1,0:T(8,128)(2,1)S(1)} %get-tuple-element.7.refs_1_, bf16[3,256,896]{2,1,0:T(8,128)(2,1)S(1)} %get-tuple-element.8.refs_2_, bf16[896,896]{1,0:T(8,128)(2,1)S(1)} %dense_basis.1.dense_ref.refs_3_, ...), custom_call_target="tpu_custom_call" | custom-call | flops 5368709120 | bytes 4194304 | tf_op jit(solution)/shard_map/pallas_call | solution.py:150
  80.6 4.6 %collective-permute-done.7.refs_9_ = bf16[2048,128]{1,0:T(8,128)(2,1)S(1)} collective-permute-done((bf16[2048,128]{1,0:T(8,128)(2,1)}, bf16[2048,128]{1,0:T(8,128)(2,1)S(1)}, u32[]{:S(2)}, u32[]{:S(2)}) %collective-permute-start.7) | collective-permute-done | bytes 524320 | tf_op jit(solution)/shard_map/ppermute | solution.py:378
  85.2 0.5 collective-permute-start.9
  85.7 8.1 %collective-permute-done.3.refs_5_ = bf16[2048,128]{1,0:T(8,128)(2,1)S(1)} collective-permute-done((bf16[2048,128]{1,0:T(8,128)(2,1)}, bf16[2048,128]{1,0:T(8,128)(2,1)S(1)}, u32[]{:S(2)}, u32[]{:S(2)}) %collective-permute-start.3) | collective-permute-done | bytes 524320 | tf_op jit(solution)/shard_map/ppermute | solution.py:378
  93.8 5.4 %shard_map.65.refs_0_ = bf16[1024,2688]{1,0:T(8,128)(2,1)S(1)} custom-call(s32[3]{0:T(128)S(1)} %pad_add_fusion.where_ref.core_ref.refs_0_, bf16[256,2048]{1,0:T(8,128)(2,1)S(1)} %get-tuple-element.7.refs_1_, bf16[3,256,896]{2,1,0:T(8,128)(2,1)S(1)} %get-tuple-element.8.refs_2_, ...), custom_call_target="tpu_custom_call", output_to_operand_aliasing={{}: (9, {})} | custom-call | flops 5368709120 | bytes 4194304 | tf_op jit(solution)/shard_map/pallas_call | solution.py:150
  99.2 15.8 %shard_map.66.refs_13_ = bf16[3,2048,896]{2,1,0:T(8,128)(2,1)} custom-call(bf16[1024,2688]{1,0:T(8,128)(2,1)S(1)} %shard_map.65.refs_0_, bf16[2048,128]{1,0:T(8,128)(2,1)S(1)} %copy-done.1, bf16[2048,128]{1,0:T(8,128)(2,1)} %collective-permute-done.13.refs_5_.refs_2_, bf16[2048,128]{1,0:T(8,128)(2,1)} %collective-permute-done.14.refs_6_.refs_3_, ...), custom_call_target="tpu_custom_call" | custom-call | flops 11274289152 | bytes 11010048 | tf_op jit(solution)/shard_map/pallas_call | solution.py:194
  115.0 25.5 %half_next.1 = bf16[3,2048,896]{2,1,0:T(8,128)(2,1)} custom-call(s32[3]{0:T(128)S(1)} %pad_add_fusion.where_ref.core_ref.refs_0_, bf16[256,2048]{1,0:T(8,128)(2,1)S(1)} %get-tuple-element.7.refs_1_, bf16[3,256,896]{2,1,0:T(8,128)(2,1)S(1)} %get-tuple-element.8.refs_2_, bf16[896,896]{1,0:T(8,128)(2,1)S(1)} %dense_basis.1.dense_ref.refs_3_, ...), custom_call_target="tpu_custom_call" | custom-call | flops 11274289152 | bytes 22020096 | tf_op jit(solution)/shard_map/half_next/pallas_call | solution.py:294
  (22 shorter events, 0.1 us)
Async XLA Ops:
  0.0 0.7 copy-start
  2.7 33.7 %all-to-all-start = ((bf16[8,16,3968]{2,1,0:T(8,128)(2,1)}), bf16[8,16,3968]{2,1,0:T(8,128)(2,1)S(1)}, u32[]{:S(2)}, u32[]{:S(2)}) async-start(bf16[8,16,3968]{2,1,0:T(8,128)(2,1)} %parcels.1), calls=%async_computation | async-start | bytes 2031616 | tf_op jit(solution)/shard_map/all_to_all | solution.py:383
  10.0 47.6 %collective-permute-start.1 = (bf16[2048,128]{1,0:T(8,128)(2,1)}, bf16[2048,128]{1,0:T(8,128)(2,1)S(1)}, u32[]{:S(2)}, u32[]{:S(2)}) collective-permute-start(bf16[2048,128]{1,0:T(8,128)(2,1)} %refs_1_.1), channel_id=1, source_target_pairs={{0,4},{1,5},{2,6},{3,7},{4,12},{5,13},{6,14},{7,15},{8,0},{9,1},{1... | collective-permute-start | bytes 1572872 | tf_op jit(solution)/shard_map/ppermute | solution.py:378
  12.0 46.9 %collective-permute-start.14 = (bf16[2048,128]{1,0:T(8,128)(2,1)}, bf16[2048,128]{1,0:T(8,128)(2,1)}, u32[]{:S(2)}, u32[]{:S(2)}) collective-permute-start(bf16[2048,128]{1,0:T(8,128)(2,1)} %refs_1_.1), channel_id=1, source_target_pairs={{0,1},{1,0},{2,3},{3,2},{4,5},{5,4},{6,7},{7,6},{8,9},{9,8},{10,11... | collective-permute-start | bytes 1572872 | tf_op jit(solution)/shard_map/ppermute | solution.py:378
  36.4 36.2 %collective-permute-start = (bf16[128,3968]{1,0:T(8,128)(2,1)S(1)}, bf16[128,3968]{1,0:T(8,128)(2,1)S(1)}, u32[]{:S(2)}, u32[]{:S(2)}) collective-permute-start(bf16[128,3968]{1,0:T(8,128)(2,1)S(1)} %bitcast.4), channel_id=1, source_target_pairs={{0,1},{1,0},{2,3},{3,2},{4,5},{5,4},{6,7},{7,6},{8,9},{9,8},{10,11... | collective-permute-start | bytes 3047432 | tf_op jit(solution)/shard_map/ppermute | solution.py:378
  36.5 22.5 %collective-permute-start.13 = (bf16[2048,128]{1,0:T(8,128)(2,1)}, bf16[2048,128]{1,0:T(8,128)(2,1)}, u32[]{:S(2)}, u32[]{:S(2)}) collective-permute-start(bf16[2048,128]{1,0:T(8,128)(2,1)} %refs_1_.1), channel_id=1, source_target_pairs={{0,2},{1,3},{2,0},{3,1},{4,6},{5,7},{6,4},{7,5},{8,10},{9,11},{10,... | collective-permute-start | bytes 1572872 | tf_op jit(solution)/shard_map/ppermute | solution.py:378
  37.5 22.9 %collective-permute-start.6 = (bf16[2048,128]{1,0:T(8,128)(2,1)}, bf16[2048,128]{1,0:T(8,128)(2,1)}, u32[]{:S(2)}, u32[]{:S(2)}) collective-permute-start(bf16[2048,128]{1,0:T(8,128)(2,1)} %refs_1_.1), channel_id=1, source_target_pairs={{4,0},{5,1},{6,2},{7,3},{12,4},{13,5},{14,6},{15,7},{0,8},{1,9},{2... | collective-permute-start | bytes 1572872 | tf_op jit(solution)/shard_map/ppermute | solution.py:378
  57.6 12.6 %collective-permute-start.10 = (bf16[2048,128]{1,0:T(8,128)(2,1)S(1)}, bf16[2048,128]{1,0:T(8,128)(2,1)S(1)}, u32[]{:S(2)}, u32[]{:S(2)}) collective-permute-start(bf16[2048,128]{1,0:T(8,128)(2,1)S(1)} %collective-permute-done.1.refs_4_.refs_5_), channel_id=1, source_target_pairs={{0,2},{1,3},{2,0},{3,1},{4,6},{5,7},{6,4},{7,5},{8,10},{9,11},{10,... | collective-permute-start | bytes 1572872 | tf_op jit(solution)/shard_map/ppermute | solution.py:378
  59.0 13.7 %collective-permute-start.2 = (bf16[2048,128]{1,0:T(8,128)(2,1)S(1)}, bf16[2048,128]{1,0:T(8,128)(2,1)}, u32[]{:S(2)}, u32[]{:S(2)}) collective-permute-start(bf16[2048,128]{1,0:T(8,128)(2,1)S(1)} %collective-permute-done.1.refs_4_.refs_5_), channel_id=1, source_target_pairs={{0,4},{1,5},{2,6},{3,7},{4,12},{5,13},{6,14},{7,15},{8,0},{9,1},{1... | collective-permute-start | bytes 1572872 | tf_op jit(solution)/shard_map/ppermute | solution.py:378
  59.0 15.0 %collective-permute-start.15 = (bf16[2048,128]{1,0:T(8,128)(2,1)}, bf16[2048,128]{1,0:T(8,128)(2,1)}, u32[]{:S(2)}, u32[]{:S(2)}) collective-permute-start(bf16[2048,128]{1,0:T(8,128)(2,1)} %collective-permute-done.13.refs_5_.refs_2_), channel_id=1, source_target_pairs={{0,1},{1,0},{2,3},{3,2},{4,5},{5,4},{6,7},{7,6},{8,9},{9,8},{10,11... | collective-permute-start | bytes 1572872 | tf_op jit(solution)/shard_map/ppermute | solution.py:378
  59.1 15.2 %copy-start.1 = (bf16[2048,128]{1,0:T(8,128)(2,1)S(1)}, bf16[2048,128]{1,0:T(8,128)(2,1)}, u32[]{:S(2)}) copy-start(bf16[2048,128]{1,0:T(8,128)(2,1)} %refs_1_.1) | copy-start | bytes 1572868
  60.5 24.7 %collective-permute-start.11 = (bf16[2048,128]{1,0:T(8,128)(2,1)S(1)}, bf16[2048,128]{1,0:T(8,128)(2,1)S(1)}, u32[]{:S(2)}, u32[]{:S(2)}) collective-permute-start(bf16[2048,128]{1,0:T(8,128)(2,1)S(1)} %collective-permute-done.1.refs_4_.refs_5_), channel_id=1, source_target_pairs={{0,1},{1,0},{2,3},{3,2},{4,5},{5,4},{6,7},{7,6},{8,9},{9,8},{10,11... | collective-permute-start | bytes 1572872 | tf_op jit(solution)/shard_map/ppermute | solution.py:378
  70.2 15.0 %collective-permute-start.7 = (bf16[2048,128]{1,0:T(8,128)(2,1)}, bf16[2048,128]{1,0:T(8,128)(2,1)S(1)}, u32[]{:S(2)}, u32[]{:S(2)}) collective-permute-start(bf16[2048,128]{1,0:T(8,128)(2,1)} %collective-permute-done.6.refs_8_), channel_id=1, source_target_pairs={{0,2},{1,3},{2,0},{3,1},{4,6},{5,7},{6,4},{7,5},{8,10},{9,11},{10,... | collective-permute-start | bytes 1572872 | tf_op jit(solution)/shard_map/ppermute | solution.py:378
  72.6 21.2 %collective-permute-start.12 = (bf16[2048,128]{1,0:T(8,128)(2,1)S(1)}, bf16[2048,128]{1,0:T(8,128)(2,1)S(1)}, u32[]{:S(2)}, u32[]{:S(2)}) collective-permute-start(bf16[2048,128]{1,0:T(8,128)(2,1)S(1)} %collective-permute-done.10.refs_5_.refs_6_), channel_id=1, source_target_pairs={{0,1},{1,0},{2,3},{3,2},{4,5},{5,4},{6,7},{7,6},{8,9},{9,8},{10,11... | collective-permute-start | bytes 1572872 | tf_op jit(solution)/shard_map/ppermute | solution.py:378
  72.6 21.2 %collective-permute-start.3 = (bf16[2048,128]{1,0:T(8,128)(2,1)}, bf16[2048,128]{1,0:T(8,128)(2,1)S(1)}, u32[]{:S(2)}, u32[]{:S(2)}) collective-permute-start(bf16[2048,128]{1,0:T(8,128)(2,1)} %collective-permute-done.2.refs_4_), channel_id=1, source_target_pairs={{0,2},{1,3},{2,0},{3,1},{4,6},{5,7},{6,4},{7,5},{8,10},{9,11},{10,... | collective-permute-start | bytes 1572872 | tf_op jit(solution)/shard_map/ppermute | solution.py:378
  74.0 41.0 %collective-permute-start.8 = (bf16[2048,128]{1,0:T(8,128)(2,1)}, bf16[2048,128]{1,0:T(8,128)(2,1)S(1)}, u32[]{:S(2)}, u32[]{:S(2)}) collective-permute-start(bf16[2048,128]{1,0:T(8,128)(2,1)} %collective-permute-done.6.refs_8_), channel_id=1, source_target_pairs={{0,1},{1,0},{2,3},{3,2},{4,5},{5,4},{6,7},{7,6},{8,9},{9,8},{10,11... | collective-permute-start | bytes 1572872 | tf_op jit(solution)/shard_map/ppermute | solution.py:378
  85.2 29.8 %collective-permute-start.4 = (bf16[2048,128]{1,0:T(8,128)(2,1)}, bf16[2048,128]{1,0:T(8,128)(2,1)S(1)}, u32[]{:S(2)}, u32[]{:S(2)}) collective-permute-start(bf16[2048,128]{1,0:T(8,128)(2,1)} %collective-permute-done.2.refs_4_), channel_id=1, source_target_pairs={{0,1},{1,0},{2,3},{3,2},{4,5},{5,4},{6,7},{7,6},{8,9},{9,8},{10,11... | collective-permute-start | bytes 1572872 | tf_op jit(solution)/shard_map/ppermute | solution.py:378
  85.2 29.8 %collective-permute-start.9 = (bf16[2048,128]{1,0:T(8,128)(2,1)S(1)}, bf16[2048,128]{1,0:T(8,128)(2,1)S(1)}, u32[]{:S(2)}, u32[]{:S(2)}) collective-permute-start(bf16[2048,128]{1,0:T(8,128)(2,1)S(1)} %collective-permute-done.7.refs_9_), channel_id=1, source_target_pairs={{0,1},{1,0},{2,3},{3,2},{4,5},{5,4},{6,7},{7,6},{8,9},{9,8},{10,11... | collective-permute-start | bytes 1572872 | tf_op jit(solution)/shard_map/ppermute | solution.py:378
  93.8 21.2 %collective-permute-start.5 = (bf16[2048,128]{1,0:T(8,128)(2,1)S(1)}, bf16[2048,128]{1,0:T(8,128)(2,1)S(1)}, u32[]{:S(2)}, u32[]{:S(2)}) collective-permute-start(bf16[2048,128]{1,0:T(8,128)(2,1)S(1)} %collective-permute-done.3.refs_5_), channel_id=1, source_target_pairs={{0,1},{1,0},{2,3},{3,2},{4,5},{5,4},{6,7},{7,6},{8,9},{9,8},{10,11... | collective-permute-start | bytes 1572872 | tf_op jit(solution)/shard_map/ppermute | solution.py:378

commit v5 on v4

--- a/solution.py
+++ b/solution.py
@@ -163,12 +163,12 @@
     )(where, *args)
 
 
-def product_kernel(first, count, *refs):
+def product_kernel(first, count, start, *refs):
     rb_ref = refs[0]
     basis_refs = refs[1 : 1 + count]
     acc_ref, out_ref = (None if first else refs[1 + count]), refs[-1]
     rows, width = out_ref.shape[1:]
-    at = pl.ds(pl.multiple_of(pl.program_id(0) * rows, rows), rows)
+    at = pl.ds(pl.multiple_of((pl.program_id(0) + start) * rows, rows), rows)
     lhs = jnp.concatenate([r[at, :] for r in basis_refs], axis=1)
     part = jnp.dot(lhs, rb_ref[...], preferred_element_type=jnp.float32)
     for q in range(QUERIES):
@@ -178,23 +178,26 @@
         out_ref[q] = own.astype(out_ref.dtype)
 
 
-def product_of(rb, bases, acc):
+def product_of(rb, bases, acc, start, steps, prior):
     units, shard = bases[0].shape
     count = len(bases)
     width = rb.shape[1] // QUERIES
-    rows = min(units, 2 * ROWS)
     first = acc is None
+    rows = min(units, ROWS if first else 2 * ROWS)
     whole = pl.BlockSpec(memory_space=pltpu.VMEM)
-    out_block = pl.BlockSpec((QUERIES, rows, width), lambda i: (0, i, 0))
+    out_block = pl.BlockSpec((QUERIES, rows, width), lambda i: (0, i + start, 0))
     in_specs = [whole] * (1 + count)
     args = [rb, *bases]
     if not first:
         in_specs.append(out_block)
         args.append(pltpu.with_memory_space_constraint(acc, pltpu.HBM))
-    return pl.pallas_call(
-        functools.partial(product_kernel, first, count),
+    if prior is not None:
+        in_specs.append(pl.BlockSpec(memory_space=pltpu.HBM))
+        args.append(prior)
+    return pl.pallas_call(
+        functools.partial(product_kernel, first, count, start),
         out_shape=pltpu.HBM((QUERIES, units, width), jnp.bfloat16),
-        grid=(units // rows,),
+        grid=(steps,),
         in_specs=in_specs,
         out_specs=out_block,
         compiler_params=pltpu.CompilerParams(
@@ -205,117 +208,8 @@
             bytes_accessed=QUERIES * units * width * (2 if first else 4),
             transcendentals=0,
         ),
+        input_output_aliases={} if prior is None else {len(args) - 1: 0},
     )(*args)
-
-
-def half_kernel(order, first, count, sources, *refs):
-    where_ref, og_ref, sel_ref, dense_ref = refs[:4]
-    basis_refs = refs[4 : 4 + count]
-    eig_ref = refs[4 + count]
-    if first:
-        acc_ref = None
-        out_ref, rgt_ref, inv_ref, rb_ref, sems = refs[5 + count :]
-    else:
-        acc_ref, out_ref, rgt_ref, inv_ref, rb_ref, sems = refs[5 + count :]
-    step = pl.program_id(0)
-    rows, width = out_ref.shape[1:]
-    shard = basis_refs[0].shape[1]
-
-    @pl.when(step == 0)
-    def _():
-        z, y, c = where_ref[0], where_ref[1], where_ref[2]
-        level_z = [
-            sum(jnp.where(z == i, v, 0) for i, v in enumerate(table)) for table in sources
-        ]
-
-        def fetch(j):
-            yy = y if j % 2 == 0 else 1 - y
-            cc = c if j % 4 < 2 else 1 - c
-            place = (level_z[j // 4] * 2 + yy) * 2 + cc
-            at = pl.ds(pl.multiple_of(place * shard, shard), shard)
-            to = pl.ds(pl.multiple_of(j * shard, shard), shard)
-            return pltpu.make_async_copy(eig_ref.at[at, :], inv_ref.at[to, :], sems.at[j])
-
-        fetches = [fetch(j) for j in range(count)]
-        for f in fetches:
-            f.start()
-        for j in range(0, count, 2):
-            basis = jnp.concatenate([r[...] for r in basis_refs[j : j + 2]], axis=1)
-            rg = jnp.dot(og_ref[...], basis, preferred_element_type=jnp.float32)
-            rgt_ref[j * shard : (j + 2) * shard, :] = rg.astype(jnp.bfloat16).T
-
-        @pl.loop(0, count // 2)
-        def _(i):
-            for j in (2 * i, 2 * i + 1):
-                to = pl.ds(pl.multiple_of(j * shard, shard), shard)
-                pltpu.make_async_copy(
-                    eig_ref.at[0:shard, :], inv_ref.at[to, :], sems.at[j]
-                ).wait()
-            at = pl.ds(pl.multiple_of(i * 2 * shard, 2 * shard), 2 * shard)
-            inv = 1.0 / inv_ref[at, :]
-            for q in range(QUERIES):
-                m = jnp.dot(rgt_ref[at, :], sel_ref[q], preferred_element_type=jnp.float32)
-                s = (m * inv).astype(jnp.bfloat16)
-                for n0, n1, k0, k1 in windows(width, order):
-                    back = lax.dot_general(
-                        s[:, k0:k1],
-                        dense_ref[n0:n1, k0:k1],
-                        (((1,), (1,)), ((), ())),
-                        preferred_element_type=jnp.float32,
-                    )
-                    rb_ref[at, q * width + n0 : q * width + n1] = back.astype(jnp.bfloat16)
-
-    at = pl.ds(pl.multiple_of(step * rows, rows), rows)
-    lhs = jnp.concatenate([r[at, :] for r in basis_refs], axis=1)
-    part = jnp.dot(lhs, rb_ref[...], preferred_element_type=jnp.float32)
-    for q in range(QUERIES):
-        own = part[:, q * width : (q + 1) * width]
-        if not first:
-            own = own + acc_ref[q].astype(jnp.float32)
-        out_ref[q] = own.astype(out_ref.dtype)
-
-
-def half_of(order, sources, where, og, sel, dense, bases, eig, acc):
-    tokens, units = og.shape
-    width = sel.shape[2]
-    shard = bases[0].shape[1]
-    count = len(bases)
-    rows = min(units, ROWS)
-    first = acc is None
-    whole = pl.BlockSpec(memory_space=pltpu.VMEM)
-    in_specs = [whole] * 3
-    in_specs += [whole] * count
-    in_specs.append(pl.BlockSpec(memory_space=pltpu.HBM))
-    out_block = pl.BlockSpec((QUERIES, rows, width), lambda i, s: (0, i, 0))
-    args = [og, sel, dense, *bases, pltpu.with_memory_space_constraint(eig, pltpu.HBM)]
-    if not first:
-        in_specs.append(out_block)
-        args.append(pltpu.with_memory_space_constraint(acc, pltpu.HBM))
-    return pl.pallas_call(
-        functools.partial(half_kernel, order, first, count, sources),
-        out_shape=pltpu.HBM((QUERIES, units, width), jnp.bfloat16),
-        grid_spec=pltpu.PrefetchScalarGridSpec(
-            num_scalar_prefetch=1,
-            grid=(units // rows,),
-            in_specs=in_specs,
-            out_specs=out_block,
-            scratch_shapes=[
-                pltpu.VMEM((count * shard, tokens), jnp.bfloat16),
-                pltpu.VMEM((count * shard, width), jnp.float32),
-                pltpu.VMEM((count * shard, QUERIES * width), jnp.bfloat16),
-                pltpu.SemaphoreType.DMA((count,)),
-            ],
-        ),
-        compiler_params=pltpu.CompilerParams(
-            dimension_semantics=("arbitrary",), vmem_limit_bytes=30 << 20
-        ),
-        cost_estimate=pl.CostEstimate(
-            flops=2 * QUERIES * width * count * shard * units,
-            bytes_accessed=QUERIES * units * width * (2 if first else 4),
-            transcendentals=0,
-        ),
-        name="half_first" if first else "half_next",
-    )(where, *args)
 
 
 def parcel_kernel(ids_ref, act_ref, grads_ref, out_ref):
@@ -403,15 +297,22 @@
         sources.append(tuple(level_z))
         level_z = [before[v] for v in level_z]
     slots = nz // 2
-    rb = None
-    for k in range(slots):
-        rb = back_of(order, sources[k], k, slots, where, og, sel, dense, levels[k], eigenvalues, rb)
-    acc = product_of(rb, [b for k in range(slots) for b in levels[k]], None)
-    rest = range(slots, nz)
-    bases = [b for k in rest for b in levels[k]]
-    return half_of(
-        order, [sources[k] for k in rest], where, og, sel, dense, bases, eigenvalues, acc
-    )
+    blocks = units // ROWS
+    cut = blocks // 2
+
+    def backs(ks):
+        rb = None
+        for slot, k in enumerate(ks):
+            rb = back_of(
+                order, sources[k], slot, slots, where, og, sel, dense, levels[k], eigenvalues, rb
+            )
+        return rb, [b for k in ks for b in levels[k]]
+
+    rb, bases = backs(range(slots))
+    acc = product_of(rb, bases, None, 0, cut, None)
+    acc = product_of(rb, bases, None, cut, blocks - cut, acc)
+    rb, bases = backs(range(slots, nz))
+    return product_of(rb, bases, acc, 0, blocks // 2, None)
 
 
 def plain(activations, out_grads, query_ids, act_basis, grad_basis, eigenvalues):
@@ -469,7 +370,7 @@
     def body(activations, out_grads, query_ids, act_basis, grad_basis, eigenvalues):
         shard = grad_basis.shape[1]
         width = act_basis.shape[0] * act_basis.shape[1]
-        if shard % LANES or width % LANES or nz % 2:
+        if shard % LANES or width % LANES or nz % 2 or grad_basis.shape[0] % (2 * ROWS):
             return plain(activations, out_grads, query_ids, act_basis, grad_basis, eigenvalues)
         return streamed(
             shape, activations, out_grads, query_ids, act_basis, grad_basis, eigenvalues

time: 141 us -> 146 us (1.035)
  Pallas kernels: 57.4 us -> 62.7 us
  waiting for transfers between devices: 67.2 us -> 65.5 us
    pallas_call x2 -> x4, Pallas kernels: 11.7 us -> 23.3 us  [back_of(): pl.pallas_call(functools.partial(back_kernel, order, source, slot), out_s...]
    pallas_call x2 -> x3, Pallas kernels: 41.3 us -> 35 us  [product_of(): pl.pallas_call(functools.partial(product_kernel, first, count, start), ou...]
    all_to_all x1, waiting for transfers between devices: 24.4 us -> 22.9 us  [streamed(): lax.all_to_all(parcels, ('z', 'y'), split_axis=0, concat_axis=0, tiled=True)]
  transfers between devices with their start and end apart: 17 -> 17, of which waited for: 6 -> 6; matrix products, arithmetic and copies ran while one was open for 0% -> 0% of each run, Pallas kernels for 21% -> 27%
where the time goes in v5:
time: 146 us
  waiting for transfers between devices  65.5 us (45%)
  Pallas kernels  62.7 us (43%)
  starting transfers between devices  16 us (11%)
    ppermute x16, waiting for transfers between devices, streamed(): move = lambda v, p: lax.ppermute(v, AXES, p)  42.6 us
    pallas_call x3, Pallas kernels, product_of(): pl.pallas_call(functools.partial(product_kernel, first, count, start), ou...  35 us
    pallas_call x4, Pallas kernels, back_of(): pl.pallas_call(functools.partial(back_kernel, order, source, slot), out_s...  23.3 us
    all_to_all x1, waiting for transfers between devices, streamed(): lax.all_to_all(parcels, ('z', 'y'), split_axis=0, concat_axis=0, tiled=True)  22.9 us
    ppermute x16, starting transfers between devices, streamed(): move = lambda v, p: lax.ppermute(v, AXES, p)  8.67 us
    all_to_all x1, starting transfers between devices, streamed(): lax.all_to_all(parcels, ('z', 'y'), split_axis=0, concat_axis=0, tiled=True)  7.31 us
  transfers between devices with their start and end apart: 17, of which 6 were waited for; matrix products, arithmetic and copies ran while one was open for 0% of the time, Pallas kernels for 27%

profile of v5, /device:TPU:0, one launch (start us, length us, event | category | flops | bytes accessed | tf_op | source)
XLA Modules:
  0.0 145.9 jit_solution(7266820045147814489)
XLA Ops:
  0.0 0.7 copy-done
  0.7 2.1 %parcels.1 = bf16[8,16,3968]{2,1,0:T(8,128)(2,1)} custom-call(s32[16]{0:T(128)S(1)} %copy-done, bf16[16,14336]{1,0:T(8,128)(2,1)} %act_ref.1, bf16[16,2048]{1,0:T(8,128)(2,1)} %grads_ref.1), custom_call_target="tpu_custom_call" | custom-call | tf_op jit(solution)/shard_map/parcels/pallas_call | solution.py:233
  2.7 7.3 %all-to-all-start = ((bf16[8,16,3968]{2,1,0:T(8,128)(2,1)}), bf16[8,16,3968]{2,1,0:T(8,128)(2,1)S(1)}, u32[]{:S(2)}, u32[]{:S(2)}) async-start(bf16[8,16,3968]{2,1,0:T(8,128)(2,1)} %parcels.1), calls=%async_computation | async-start | bytes 2031616 | tf_op jit(solution)/shard_map/all_to_all | solution.py:277
  10.0 2.0 %collective-permute-start.5 = (bf16[2048,128]{1,0:T(8,128)(2,1)}, bf16[2048,128]{1,0:T(8,128)(2,1)S(1)}, u32[]{:S(2)}, u32[]{:S(2)}) collective-permute-start(bf16[2048,128]{1,0:T(8,128)(2,1)} %refs_1_.3), channel_id=1, source_target_pairs={{0,4},{1,5},{2,6},{3,7},{4,12},{5,13},{6,14},{7,15},{8,0},{9,1},{1... | collective-permute-start | bytes 1572872 | tf_op jit(solution)/shard_map/ppermute | solution.py:272
  12.0 1.5 %collective-permute-start.13 = (bf16[2048,128]{1,0:T(8,128)(2,1)}, bf16[2048,128]{1,0:T(8,128)(2,1)}, u32[]{:S(2)}, u32[]{:S(2)}) collective-permute-start(bf16[2048,128]{1,0:T(8,128)(2,1)} %refs_1_.3), channel_id=1, source_target_pairs={{0,2},{1,3},{2,0},{3,1},{4,6},{5,7},{6,4},{7,5},{8,10},{9,11},{10,... | collective-permute-start | bytes 1572872 | tf_op jit(solution)/shard_map/ppermute | solution.py:272
  13.5 22.9 %all-to-all-done = bf16[8,16,3968]{2,1,0:T(8,128)(2,1)S(1)} async-done(((bf16[8,16,3968]{2,1,0:T(8,128)(2,1)}), bf16[8,16,3968]{2,1,0:T(8,128)(2,1)S(1)}, u32[]{:S(2)}, u32[]{:S(2)}) %all-to-all-start) | async-done | bytes 1015840 | tf_op jit(solution)/shard_map/all_to_all | solution.py:277
  37.0 20.6 %collective-permute-done.5.refs_4_.refs_5_ = bf16[2048,128]{1,0:T(8,128)(2,1)S(1)} collective-permute-done((bf16[2048,128]{1,0:T(8,128)(2,1)}, bf16[2048,128]{1,0:T(8,128)(2,1)S(1)}, u32[]{:S(2)}, u32[]{:S(2)}) %collective-permute-start.5) | collective-permute-done | bytes 524320 | tf_op jit(solution)/shard_map/ppermute | solution.py:272
  57.6 1.4 collective-permute-start.10
  59.0 0.8 copy-done.2
  59.9 1.3 dense_basis.1.dense_ref.refs_3_
  61.2 0.6 collective-permute-start.11
  61.8 8.5 %collective-permute-done.10.refs_5_.refs_6_ = bf16[2048,128]{1,0:T(8,128)(2,1)} collective-permute-done((bf16[2048,128]{1,0:T(8,128)(2,1)S(1)}, bf16[2048,128]{1,0:T(8,128)(2,1)}, u32[]{:S(2)}, u32[]{:S(2)}) %collective-permute-start.10) | collective-permute-done | bytes 524320 | tf_op jit(solution)/shard_map/ppermute | solution.py:272
  70.3 1.7 %collective-permute-start.2 = (bf16[2048,128]{1,0:T(8,128)(2,1)S(1)}, bf16[2048,128]{1,0:T(8,128)(2,1)S(1)}, u32[]{:S(2)}, u32[]{:S(2)}) collective-permute-start(bf16[2048,128]{1,0:T(8,128)(2,1)S(1)} %collective-permute-done.1.refs_4_.refs_5_), channel_id=1, source_target_pairs={{0,2},{1,3},{2,0},{3,1},{4,6},{5,7},{6,4},{7,5},{8,10},{9,11},{10,... | collective-permute-start | bytes 1572872 | tf_op jit(solution)/shard_map/ppermute | solution.py:272
  72.0 0.6 collective-permute-done.6.refs_4_.refs_1_
  72.9 1.1 tokens.1
  74.3 6.1 %shard_map.66.refs_9_ = bf16[1024,2688]{1,0:T(8,128)(2,1)S(1)} custom-call(s32[3]{0:T(128)S(1)} %pad_add_fusion.where_ref.core_ref.refs_0_, bf16[256,2048]{1,0:T(8,128)(2,1)S(1)} %get-tuple-element.7.refs_1_, bf16[3,256,896]{2,1,0:T(8,128)(2,1)S(1)} %get-tuple-element.8.refs_2_, bf16[896,896]{1,0:T(8,128)(2,1)S(1)} %dense_basis.1.dense_ref.refs_3_, ...), custom_call_target="tpu_custom_call" | custom-call | flops 5368709120 | bytes 4194304 | tf_op jit(solution)/shard_map/pallas_call | solution.py:150
  80.8 4.3 %collective-permute-done.2.refs_5_.refs_6_ = bf16[2048,128]{1,0:T(8,128)(2,1)S(1)} collective-permute-done((bf16[2048,128]{1,0:T(8,128)(2,1)S(1)}, bf16[2048,128]{1,0:T(8,128)(2,1)S(1)}, u32[]{:S(2)}, u32[]{:S(2)}) %collective-permute-start.2) | collective-permute-done | bytes 524320 | tf_op jit(solution)/shard_map/ppermute | solution.py:272
  85.1 8.5 %collective-permute-done.7.refs_5_.refs_2_ = bf16[2048,128]{1,0:T(8,128)(2,1)S(1)} collective-permute-done((bf16[2048,128]{1,0:T(8,128)(2,1)}, bf16[2048,128]{1,0:T(8,128)(2,1)S(1)}, u32[]{:S(2)}, u32[]{:S(2)}) %collective-permute-start.7) | collective-permute-done | bytes 524320 | tf_op jit(solution)/shard_map/ppermute | solution.py:272
  93.6 5.9 %shard_map.67.refs_0_ = bf16[1024,2688]{1,0:T(8,128)(2,1)S(1)} custom-call(s32[3]{0:T(128)S(1)} %pad_add_fusion.where_ref.core_ref.refs_0_, bf16[256,2048]{1,0:T(8,128)(2,1)S(1)} %get-tuple-element.7.refs_1_, bf16[3,256,896]{2,1,0:T(8,128)(2,1)S(1)} %get-tuple-element.8.refs_2_, ...), custom_call_target="tpu_custom_call", output_to_operand_aliasing={{}: (9, {})} | custom-call | flops 5368709120 | bytes 4194304 | tf_op jit(solution)/shard_map/pallas_call | solution.py:150
  99.5 9.4 %shard_map.68.refs_9_ = bf16[3,2048,896]{2,1,0:T(8,128)(2,1)} custom-call(bf16[1024,2688]{1,0:T(8,128)(2,1)S(1)} %shard_map.67.refs_0_, bf16[2048,128]{1,0:T(8,128)(2,1)S(1)} %copy-done.1, bf16[2048,128]{1,0:T(8,128)(2,1)} %collective-permute-done.13.refs_5_.refs_2_, bf16[2048,128]{1,0:T(8,128)(2,1)S(1)} %copy-done.3, ...), custom_call_target="tpu_custom_call" | custom-call | flops 11274289152 | bytes 11010048 | tf_op jit(solution)/shard_map/pallas_call | solution.py:197
  108.9 9.3 %shard_map.69.refs_9_ = bf16[3,2048,896]{2,1,0:T(8,128)(2,1)} custom-call(bf16[1024,2688]{1,0:T(8,128)(2,1)S(1)} %shard_map.67.refs_0_, bf16[2048,128]{1,0:T(8,128)(2,1)S(1)} %copy-done.1, bf16[2048,128]{1,0:T(8,128)(2,1)} %collective-permute-done.13.refs_5_.refs_2_, bf16[2048,128]{1,0:T(8,128)(2,1)S(1)} %copy-done.3, ...), custom_call_target="tpu_custom_call", output_to_operand_aliasing={{}: (9, {})} | custom-call | flops 11274289152 | bytes 11010048 | tf_op jit(solution)/shard_map/pallas_call | solution.py:197
  118.3 5.9 %shard_map.64.refs_9_ = bf16[1024,2688]{1,0:T(8,128)(2,1)S(1)} custom-call(s32[3]{0:T(128)S(1)} %pad_add_fusion.where_ref.core_ref.refs_0_, bf16[256,2048]{1,0:T(8,128)(2,1)S(1)} %get-tuple-element.7.refs_1_, bf16[3,256,896]{2,1,0:T(8,128)(2,1)S(1)} %get-tuple-element.8.refs_2_, bf16[896,896]{1,0:T(8,128)(2,1)S(1)} %dense_basis.1.dense_ref.refs_3_, ...), custom_call_target="tpu_custom_call" | custom-call | flops 5368709120 | bytes 4194304 | tf_op jit(solution)/shard_map/pallas_call | solution.py:150
  124.2 5.4 %shard_map.65.refs_0_ = bf16[1024,2688]{1,0:T(8,128)(2,1)S(1)} custom-call(s32[3]{0:T(128)S(1)} %pad_add_fusion.where_ref.core_ref.refs_0_, bf16[256,2048]{1,0:T(8,128)(2,1)S(1)} %get-tuple-element.7.refs_1_, bf16[3,256,896]{2,1,0:T(8,128)(2,1)S(1)} %get-tuple-element.8.refs_2_, ...), custom_call_target="tpu_custom_call", output_to_operand_aliasing={{}: (9, {})} | custom-call | flops 5368709120 | bytes 4194304 | tf_op jit(solution)/shard_map/pallas_call | solution.py:150
  129.6 16.3 %shard_map.70 = bf16[3,2048,896]{2,1,0:T(8,128)(2,1)} custom-call(bf16[1024,2688]{1,0:T(8,128)(2,1)S(1)} %shard_map.65.refs_0_, bf16[2048,128]{1,0:T(8,128)(2,1)} %collective-permute-done.6.refs_4_.refs_1_, bf16[2048,128]{1,0:T(8,128)(2,1)S(1)} %collective-permute-done.7.refs_5_.refs_2_, bf16[2048,128]{1,0:T(8,128)(2,1)S(1)} %collective-permute-done.8.refs_6_.refs_3_, ...), custom_call_target="tpu_custom_call" | custom-call | flops 11274289152 | bytes 22020096 | tf_op jit(solution)/shard_map/pallas_call | solution.py:197
  (29 shorter events, 1.6 us)
Async XLA Ops:
  0.0 0.7 copy-start
  2.7 33.7 %all-to-all-start = ((bf16[8,16,3968]{2,1,0:T(8,128)(2,1)}), bf16[8,16,3968]{2,1,0:T(8,128)(2,1)S(1)}, u32[]{:S(2)}, u32[]{:S(2)}) async-start(bf16[8,16,3968]{2,1,0:T(8,128)(2,1)} %parcels.1), calls=%async_computation | async-start | bytes 2031616 | tf_op jit(solution)/shard_map/all_to_all | solution.py:277
  10.0 47.5 %collective-permute-start.5 = (bf16[2048,128]{1,0:T(8,128)(2,1)}, bf16[2048,128]{1,0:T(8,128)(2,1)S(1)}, u32[]{:S(2)}, u32[]{:S(2)}) collective-permute-start(bf16[2048,128]{1,0:T(8,128)(2,1)} %refs_1_.3), channel_id=1, source_target_pairs={{0,4},{1,5},{2,6},{3,7},{4,12},{5,13},{6,14},{7,15},{8,0},{9,1},{1... | collective-permute-start | bytes 1572872 | tf_op jit(solution)/shard_map/ppermute | solution.py:272
  12.0 46.9 %collective-permute-start.13 = (bf16[2048,128]{1,0:T(8,128)(2,1)}, bf16[2048,128]{1,0:T(8,128)(2,1)}, u32[]{:S(2)}, u32[]{:S(2)}) collective-permute-start(bf16[2048,128]{1,0:T(8,128)(2,1)} %refs_1_.3), channel_id=1, source_target_pairs={{0,2},{1,3},{2,0},{3,1},{4,6},{5,7},{6,4},{7,5},{8,10},{9,11},{10,... | collective-permute-start | bytes 1572872 | tf_op jit(solution)/shard_map/ppermute | solution.py:272
  36.4 36.2 %collective-permute-start = (bf16[128,3968]{1,0:T(8,128)(2,1)S(1)}, bf16[128,3968]{1,0:T(8,128)(2,1)S(1)}, u32[]{:S(2)}, u32[]{:S(2)}) collective-permute-start(bf16[128,3968]{1,0:T(8,128)(2,1)S(1)} %bitcast.4), channel_id=1, source_target_pairs={{0,1},{1,0},{2,3},{3,2},{4,5},{5,4},{6,7},{7,6},{8,9},{9,8},{10,11... | collective-permute-start | bytes 3047432 | tf_op jit(solution)/shard_map/ppermute | solution.py:272
  36.5 22.5 %collective-permute-start.14 = (bf16[2048,128]{1,0:T(8,128)(2,1)}, bf16[2048,128]{1,0:T(8,128)(2,1)S(1)}, u32[]{:S(2)}, u32[]{:S(2)}) collective-permute-start(bf16[2048,128]{1,0:T(8,128)(2,1)} %refs_1_.3), channel_id=1, source_target_pairs={{0,1},{1,0},{2,3},{3,2},{4,5},{5,4},{6,7},{7,6},{8,9},{9,8},{10,11... | collective-permute-start | bytes 1572872 | tf_op jit(solution)/shard_map/ppermute | solution.py:272
  37.0 24.2 %collective-permute-start.1 = (bf16[2048,128]{1,0:T(8,128)(2,1)}, bf16[2048,128]{1,0:T(8,128)(2,1)S(1)}, u32[]{:S(2)}, u32[]{:S(2)}) collective-permute-start(bf16[2048,128]{1,0:T(8,128)(2,1)} %refs_1_.3), channel_id=1, source_target_pairs={{4,0},{5,1},{6,2},{7,3},{12,4},{13,5},{14,6},{15,7},{0,8},{1,9},{2... | collective-permute-start | bytes 1572872 | tf_op jit(solution)/shard_map/ppermute | solution.py:272
  57.6 12.7 %collective-permute-start.10 = (bf16[2048,128]{1,0:T(8,128)(2,1)S(1)}, bf16[2048,128]{1,0:T(8,128)(2,1)}, u32[]{:S(2)}, u32[]{:S(2)}) collective-permute-start(bf16[2048,128]{1,0:T(8,128)(2,1)S(1)} %collective-permute-done.5.refs_4_.refs_5_), channel_id=1, source_target_pairs={{0,2},{1,3},{2,0},{3,1},{4,6},{5,7},{6,4},{7,5},{8,10},{9,11},{10,... | collective-permute-start | bytes 1572872 | tf_op jit(solution)/shard_map/ppermute | solution.py:272
  59.0 13.7 %collective-permute-start.6 = (bf16[2048,128]{1,0:T(8,128)(2,1)S(1)}, bf16[2048,128]{1,0:T(8,128)(2,1)}, u32[]{:S(2)}, u32[]{:S(2)}) collective-permute-start(bf16[2048,128]{1,0:T(8,128)(2,1)S(1)} %collective-permute-done.5.refs_4_.refs_5_), channel_id=1, source_target_pairs={{0,4},{1,5},{2,6},{3,7},{4,12},{5,13},{6,14},{7,15},{8,0},{9,1},{1... | collective-permute-start | bytes 1572872 | tf_op jit(solution)/shard_map/ppermute | solution.py:272
  59.0 0.8 copy-start.2
  59.8 14.2 %collective-permute-start.15 = (bf16[2048,128]{1,0:T(8,128)(2,1)}, bf16[2048,128]{1,0:T(8,128)(2,1)}, u32[]{:S(2)}, u32[]{:S(2)}) collective-permute-start(bf16[2048,128]{1,0:T(8,128)(2,1)} %collective-permute-done.13.refs_5_.refs_2_), channel_id=1, source_target_pairs={{0,1},{1,0},{2,3},{3,2},{4,5},{5,4},{6,7},{7,6},{8,9},{9,8},{10,11... | collective-permute-start | bytes 1572872 | tf_op jit(solution)/shard_map/ppermute | solution.py:272
  59.8 14.5 %copy-start.1 = (bf16[2048,128]{1,0:T(8,128)(2,1)S(1)}, bf16[2048,128]{1,0:T(8,128)(2,1)}, u32[]{:S(2)}) copy-start(bf16[2048,128]{1,0:T(8,128)(2,1)} %refs_1_.3) | copy-start | bytes 1572868
  59.8 14.5 %copy-start.3 = (bf16[2048,128]{1,0:T(8,128)(2,1)S(1)}, bf16[2048,128]{1,0:T(8,128)(2,1)}, u32[]{:S(2)}) copy-start(bf16[2048,128]{1,0:T(8,128)(2,1)} %copy-done.2) | copy-start | bytes 1572868
  61.2 19.2 %collective-permute-start.11 = (bf16[2048,128]{1,0:T(8,128)(2,1)S(1)}, bf16[2048,128]{1,0:T(8,128)(2,1)S(1)}, u32[]{:S(2)}, u32[]{:S(2)}) collective-permute-start(bf16[2048,128]{1,0:T(8,128)(2,1)S(1)} %collective-permute-done.5.refs_4_.refs_5_), channel_id=1, source_target_pairs={{0,1},{1,0},{2,3},{3,2},{4,5},{5,4},{6,7},{7,6},{8,9},{9,8},{10,11... | collective-permute-start | bytes 1572872 | tf_op jit(solution)/shard_map/ppermute | solution.py:272
  70.3 14.8 %collective-permute-start.2 = (bf16[2048,128]{1,0:T(8,128)(2,1)S(1)}, bf16[2048,128]{1,0:T(8,128)(2,1)S(1)}, u32[]{:S(2)}, u32[]{:S(2)}) collective-permute-start(bf16[2048,128]{1,0:T(8,128)(2,1)S(1)} %collective-permute-done.1.refs_4_.refs_5_), channel_id=1, source_target_pairs={{0,2},{1,3},{2,0},{3,1},{4,6},{5,7},{6,4},{7,5},{8,10},{9,11},{10,... | collective-permute-start | bytes 1572872 | tf_op jit(solution)/shard_map/ppermute | solution.py:272
  72.6 21.0 %collective-permute-start.12 = (bf16[2048,128]{1,0:T(8,128)(2,1)}, bf16[2048,128]{1,0:T(8,128)(2,1)S(1)}, u32[]{:S(2)}, u32[]{:S(2)}) collective-permute-start(bf16[2048,128]{1,0:T(8,128)(2,1)} %collective-permute-done.10.refs_5_.refs_6_), channel_id=1, source_target_pairs={{0,1},{1,0},{2,3},{3,2},{4,5},{5,4},{6,7},{7,6},{8,9},{9,8},{10,11... | collective-permute-start | bytes 1572872 | tf_op jit(solution)/shard_map/ppermute | solution.py:272
  72.6 20.9 %collective-permute-start.7 = (bf16[2048,128]{1,0:T(8,128)(2,1)}, bf16[2048,128]{1,0:T(8,128)(2,1)S(1)}, u32[]{:S(2)}, u32[]{:S(2)}) collective-permute-start(bf16[2048,128]{1,0:T(8,128)(2,1)} %collective-permute-done.6.refs_4_.refs_1_), channel_id=1, source_target_pairs={{0,2},{1,3},{2,0},{3,1},{4,6},{5,7},{6,4},{7,5},{8,10},{9,11},{10,... | collective-permute-start | bytes 1572872 | tf_op jit(solution)/shard_map/ppermute | solution.py:272
  74.0 50.2 %collective-permute-start.3 = (bf16[2048,128]{1,0:T(8,128)(2,1)S(1)}, bf16[2048,128]{1,0:T(8,128)(2,1)S(1)}, u32[]{:S(2)}, u32[]{:S(2)}) collective-permute-start(bf16[2048,128]{1,0:T(8,128)(2,1)S(1)} %collective-permute-done.1.refs_4_.refs_5_), channel_id=1, source_target_pairs={{0,1},{1,0},{2,3},{3,2},{4,5},{5,4},{6,7},{7,6},{8,9},{9,8},{10,11... | collective-permute-start | bytes 1572872 | tf_op jit(solution)/shard_map/ppermute | solution.py:272
  80.4 37.8 %collective-permute-start.8 = (bf16[2048,128]{1,0:T(8,128)(2,1)}, bf16[2048,128]{1,0:T(8,128)(2,1)S(1)}, u32[]{:S(2)}, u32[]{:S(2)}) collective-permute-start(bf16[2048,128]{1,0:T(8,128)(2,1)} %collective-permute-done.6.refs_4_.refs_1_), channel_id=1, source_target_pairs={{0,1},{1,0},{2,3},{3,2},{4,5},{5,4},{6,7},{7,6},{8,9},{9,8},{10,11... | collective-permute-start | bytes 1572872 | tf_op jit(solution)/shard_map/ppermute | solution.py:272
  85.1 39.1 %collective-permute-start.4 = (bf16[2048,128]{1,0:T(8,128)(2,1)S(1)}, bf16[2048,128]{1,0:T(8,128)(2,1)S(1)}, u32[]{:S(2)}, u32[]{:S(2)}) collective-permute-start(bf16[2048,128]{1,0:T(8,128)(2,1)S(1)} %collective-permute-done.2.refs_5_.refs_6_), channel_id=1, source_target_pairs={{0,1},{1,0},{2,3},{3,2},{4,5},{5,4},{6,7},{7,6},{8,9},{9,8},{10,11... | collective-permute-start | bytes 1572872 | tf_op jit(solution)/shard_map/ppermute | solution.py:272
  93.6 24.7 %collective-permute-start.9 = (bf16[2048,128]{1,0:T(8,128)(2,1)S(1)}, bf16[2048,128]{1,0:T(8,128)(2,1)S(1)}, u32[]{:S(2)}, u32[]{:S(2)}) collective-permute-start(bf16[2048,128]{1,0:T(8,128)(2,1)S(1)} %collective-permute-done.7.refs_5_.refs_2_), channel_id=1, source_target_pairs={{0,1},{1,0},{2,3},{3,2},{4,5},{5,4},{6,7},{7,6},{8,9},{9,8},{10,11... | collective-permute-start | bytes 1572872 | tf_op jit(solution)/shard_map/ppermute | solution.py:272
